TPU v7x, 512 devices: a whole 4x4x16 slice. The times are simulated.
512 devices in a mesh: lat: 16 (over z), lon: 32 (over x, y, core).
Axes of the slice: x: 4, y: 4, z: 16, core: 2. Of those that a mesh axis runs over, the one named last changes fastest.
Arguments:
- diffusivity: float32 [10, 512, 4096], P(None, 'lat', 'lon'), may hold values from 0.03 to 0.24
- land_mask: int32 [512, 4096], P('lat', 'lon'), may hold values 0 or 1
- obs_weights: bfloat16 [2, 8, 512, 4096], P(None, None, 'lat', 'lon'), may hold values from -0.09375 to 0.09375
- innovation: float32 [2, 16, 32, 8], P(None, 'lat', 'lon'), may hold values from -192 to 192
- precision_weights: float32 [2, 16, 32, 8], P(None, 'lat', 'lon'), may hold values from 0.5 to 4
- obs_count: int32 [16, 32], P('lat', 'lon'), may hold values from 2 to 8, as said below
Outputs:
- control: float32 [10, 512, 4096], P(None, 'lat', 'lon')
- increment: float32 [10, 512, 4096], P(None, 'lat', 'lon')
Inputs may be any that keep to these rules, and one draw needn't show every extreme that they name: Tile (a, b) has valid observations in slots 0 to obs_count[a, b] - 1; some tile has 8.
All inputs are finite; a program needn't handle non-finite values. No bound on the sum of `land_mask` on one device may be relied on, other than what follows from the above.
Results may differ from a plain program's by a relative error of at most 0.0049.
Values sent between devices are 32-bit elements; how exact they have to be, the bound alone decides.
No kernel may reach another device: no remote copies, remote signals or barrier semaphores. Data moves between devices by JAX's collectives and lax.ppermute only.
A program may use at most 64 MiB of HBM per device.

v0:
```python
import jax
import jax.numpy as jnp
from jax import lax
from jax.sharding import PartitionSpec as P

NCAT = 5
STEPS = 6
ITERS = 2


def extended(block, sides, width):
    for axis, dim in sides:
        count = lax.axis_size(axis)
        forward = [(i, i + 1) for i in range(count - 1)]
        forward.append((count - 1, 0))
        backward = [(target, source) for source, target in forward]
        low = lax.ppermute(
            lax.slice_in_dim(block, block.shape[dim] - width, None, axis=dim), axis, forward
        )
        high = lax.ppermute(lax.slice_in_dim(block, 0, width, axis=dim), axis, backward)
        block = jnp.concatenate([low, block, high], axis=dim)
    return block


def advance(padded, east_face, north_face):
    center = padded[:, 1:-1, 1:-1]
    change = east_face[:, 1:-1, 1:] * (padded[:, 1:-1, 2:] - center)
    change = change + east_face[:, 1:-1, :-1] * (padded[:, 1:-1, :-2] - center)
    change = change + north_face[:, 1:, 1:-1] * (padded[:, 2:, 1:-1] - center)
    change = change + north_face[:, :-1, 1:-1] * (padded[:, :-2, 1:-1] - center)
    return center + change


def face_pair(grown):
    scaled = grown[:-1]
    wet = grown[-1:]
    east = 0.5 * (scaled[:, :, :-1] * wet[:, :, 1:] + scaled[:, :, 1:] * wet[:, :, :-1])
    north = 0.5 * (scaled[:, :-1, :] * wet[:, 1:, :] + scaled[:, 1:, :] * wet[:, :-1, :])
    return (east, north)


def squares(residual):
    return lax.psum(jnp.sum(residual * residual), ("lat", "lon"))


def per_device(diffusivity, land_mask, obs_weights, innovation, precision_weights, obs_count):
    ocean = land_mask.astype(jnp.float32)
    width = 1
    stacked = jnp.concatenate([diffusivity * ocean[None], ocean[None]], axis=0)
    grown = extended(stacked, (("lat", 1), ("lon", 2)), width)
    rows = grown.shape[1]
    lat_count = lax.axis_size("lat")
    lat_place = lax.axis_index("lat")
    row_ids = lax.broadcasted_iota(jnp.int32, (1, rows, 1), 1)
    outside = (lat_place == 0) & (row_ids < width) | (lat_place == lat_count - 1) & (
        row_ids >= rows - width
    )
    grown = jnp.where(outside, 0.0, grown)
    east, north = face_pair(grown)

    def extend(field):
        return extended(field, (("lat", 1), ("lon", 2)), width)

    def diffuse(field):
        for number in range(STEPS):
            field = advance(extend(field), east, north)
        return field

    def cover(field):
        return ocean[None] * diffuse(field)

    def cover_adjoint(field):
        return diffuse(ocean[None] * field)

    tile_rows, tile_cols = ocean.shape
    flat_weights = obs_weights.reshape(2, obs_weights.shape[1], tile_rows * tile_cols)
    slots = lax.broadcasted_iota(jnp.int32, innovation.shape, 3)
    keep = jnp.where(slots < obs_count[0, 0], precision_weights, 0.0)

    def spread(weighted):
        rounded = weighted.reshape(2, -1).astype(jnp.bfloat16)
        back = jnp.einsum("fok,fo->fk", flat_weights, rounded, preferred_element_type=jnp.float32)
        return jnp.repeat(back.reshape(2, tile_rows, tile_cols), NCAT, axis=0)

    right = cover_adjoint(spread(keep * innovation))
    control = jnp.zeros_like(right)
    residual = right
    direction = right
    norm_now = squares(residual)
    for number in range(ITERS):
        total = (
            cover(direction).reshape(2, NCAT, tile_rows, tile_cols).sum(axis=1).astype(jnp.bfloat16)
        )
        seen = jnp.einsum(
            "fok,fk->fo", flat_weights, total.reshape(2, -1), preferred_element_type=jnp.float32
        )
        image = direction + cover_adjoint(spread(keep * seen.reshape(innovation.shape)))
        alpha = norm_now / lax.psum(jnp.sum(direction * image), ("lat", "lon"))
        control = control + alpha * direction
        residual = residual - alpha * image
        if number + 1 < ITERS:
            norm_next = squares(residual)
            direction = residual + norm_next / norm_now * direction
            norm_now = norm_next
    return (control, cover(control))


def solution(mesh):
    return jax.shard_map(
        per_device,
        mesh=mesh,
        in_specs=(
            P(None, "lat", "lon"),
            P("lat", "lon"),
            P(None, None, "lat", "lon"),
            P(None, "lat", "lon", None),
            P(None, "lat", "lon", None),
            P("lat", "lon"),
        ),
        out_specs=(P(None, "lat", "lon"), P(None, "lat", "lon")),
        check_vma=False,
    )
```

profile of v0, /device:TPU:1, one launch (start us, length us, event | category | flops | bytes accessed | tf_op | source)
XLA Modules:
  0.0 1112.9 jit_solution(14542681047439211866)
XLA Ops:
  4.0 12.0 %collective-permute-start.5 = (f32[10,1,128]{2,1,0:T(1,128)S(1)}, f32[10,1,128]{2,1,0:T(1,128)S(1)}, u32[]{:S(2)}, u32[]{:S(2)}) collective-permute-start(f32[10,1,128]{2,1,0:T(1,128)S(1)} %get-tuple-element.157), channel_id=1, source_target_pairs={{32,0},{64,32},{96,64},{128,96},{160,128},{192,160},{224,192},{256... | collective-permute-start | bytes 15368 | tf_op jit(solution)/shard_map/ppermute | solution.py:20
  19.8 4.6 collective-permute-start.1
  25.3 5.2 collective-permute-start.2
  32.5 5.8 collective-permute-start.6
  43.3 5.1 collective-permute-start.9
  50.4 3.6 collective-permute-done.8
  54.2 9.4 collective-permute-start.10
  76.2 8.9 collective-permute-start.14
  97.7 8.9 collective-permute-start.18
  119.7 9.1 collective-permute-start.22
  142.0 9.1 collective-permute-start.26
  158.0 3.4 collective-permute-start.28
  163.7 8.9 collective-permute-start.30
  185.3 8.9 collective-permute-start.34
  207.0 9.1 collective-permute-start.38
  229.3 9.1 collective-permute-start.42
  251.1 8.9 collective-permute-start.46
  272.6 8.9 collective-permute-start.50
  288.9 3.4 collective-permute-start.52
  294.6 8.9 collective-permute-start.54
  316.1 8.9 collective-permute-start.58
  337.6 8.9 collective-permute-start.62
  359.1 8.9 collective-permute-start.66
  380.6 9.1 collective-permute-start.70
  402.9 9.1 collective-permute-start.74
  417.6 102.3 %all-reduce = (f32[]{:T(128)}, f32[]{:T(128)}) all-reduce(f32[]{:T(128)} %get-tuple-element.3, f32[]{:T(128)} %get-tuple-element.2), channel_id=1, replica_groups=mesh['lat'=16,'lon'=32] {'lat','lon'}, use_global_device_ids=true, to_apply=%region_1.2 | all-reduce | flops 2 | bytes 16 | tf_op jit(solution)/shard_map/psum | solution.py:43
  521.9 100.5 %psum.30 = f32[]{:T(128)} all-reduce(f32[]{:T(128)} %multiply_reduce_fusion), channel_id=1, replica_groups=mesh['lat'=16,'lon'=32] {'lat','lon'}, use_global_device_ids=true, to_apply=%region_6.7 | all-reduce | flops 1 | bytes 8 | tf_op jit(solution)/shard_map/psum | solution.py:43
  632.2 4.0 collective-permute-start.78
  649.9 8.3 collective-permute-start.82
  671.0 9.1 collective-permute-start.86
  692.8 8.9 collective-permute-start.90
  714.8 9.1 collective-permute-start.94
  736.6 8.9 collective-permute-start.98
  758.9 9.1 collective-permute-start.102
  780.7 8.9 collective-permute-start.106
  802.7 9.1 collective-permute-start.110
  824.4 8.9 collective-permute-start.114
  846.0 8.9 collective-permute-start.118
  867.5 8.9 collective-permute-start.122
  881.9 102.3 %psum.31 = f32[]{:T(128)} all-reduce(f32[]{:T(128)} %fusion.4), channel_id=1, replica_groups=mesh['lat'=16,'lon'=32] {'lat','lon'}, use_global_device_ids=true, to_apply=%region_9.10 | all-reduce | flops 1 | bytes 8 | tf_op jit(solution)/shard_map/psum | solution.py:98
  985.6 3.7 collective-permute-start.125
  991.2 3.6 collective-permute-done.124
  995.0 3.9 collective-permute-start.126
  1012.8 8.1 collective-permute-start.130
  1033.5 8.9 collective-permute-start.134
  1055.0 8.9 collective-permute-start.138
  1076.5 9.0 collective-permute-start.142
  1098.1 9.1 collective-permute-start.146
  (439 shorter events, 446.7 us)
Async XLA Ops:
  4.0 20.4 %collective-permute-start.5 = (f32[10,1,128]{2,1,0:T(1,128)S(1)}, f32[10,1,128]{2,1,0:T(1,128)S(1)}, u32[]{:S(2)}, u32[]{:S(2)}) collective-permute-start(f32[10,1,128]{2,1,0:T(1,128)S(1)} %get-tuple-element.157), channel_id=1, source_target_pairs={{32,0},{64,32},{96,64},{128,96},{160,128},{192,160},{224,192},{256... | collective-permute-start | bytes 15368 | tf_op jit(solution)/shard_map/ppermute | solution.py:20
  15.9 8.5 collective-permute-start.4
  17.9 6.6 collective-permute-start
  25.3 15.0 %collective-permute-start.2 = (f32[11,34,1]{2,1,0:T(8,128)S(1)}, f32[11,34,1]{2,1,0:T(8,128)S(1)}, u32[]{:S(2)}, u32[]{:S(2)}) collective-permute-start(f32[11,34,1]{2,1,0:T(8,128)S(1)} %get-tuple-element.11), channel_id=1, source_target_pairs={{0,1},{1,2},{2,3},{3,4},{4,5},{5,6},{6,7},{7,8},{8,9},{9,10},{10,1... | collective-permute-start | bytes 4496 | tf_op jit(solution)/shard_map/ppermute | solution.py:17
  30.5 9.8 collective-permute-start.3
  32.5 8.4 collective-permute-start.6
  43.3 7.1 collective-permute-start.9
  48.4 5.6 collective-permute-start.8
  54.2 11.3 %collective-permute-start.10 = (f32[10,34,1]{2,1,0:T(8,128)S(1)}, f32[10,34,1]{2,1,0:T(8,128)S(1)}, u32[]{:S(2)}, u32[]{:S(2)}) collective-permute-start(f32[10,34,1]{2,1,0:T(8,128)S(1)} %get-tuple-element.81), channel_id=1, source_target_pairs={{1,0},{2,1},{3,2},{4,3},{5,4},{6,5},{7,6},{8,7},{9,8},{10,9},{11,1... | collective-permute-start | bytes 4088 | tf_op jit(solution)/shard_map/ppermute | solution.py:20
  70.5 5.6 collective-permute-start.12
  76.2 10.8 collective-permute-start.14
  92.0 5.6 collective-permute-start.16
  97.7 10.8 collective-permute-start.18
  119.7 11.1 collective-permute-start.22
  142.0 11.1 collective-permute-start.26
  163.7 10.8 collective-permute-start.30
  185.3 10.8 collective-permute-start.34
  207.0 11.1 collective-permute-start.38
  229.3 11.1 collective-permute-start.42
  251.1 10.8 collective-permute-start.46
  272.6 10.8 collective-permute-start.50
  294.6 10.8 collective-permute-start.54
  316.1 11.0 collective-permute-start.58
  337.6 10.8 collective-permute-start.62
  359.1 10.8 collective-permute-start.66
  380.6 11.0 collective-permute-start.70
  402.9 11.1 collective-permute-start.74
  632.2 8.4 collective-permute-start.78
  636.2 5.6 collective-permute-start.79
  649.9 10.2 collective-permute-start.82
  671.0 11.1 collective-permute-start.86
  692.8 10.8 collective-permute-start.90
  714.8 11.1 collective-permute-start.94
  736.6 10.9 collective-permute-start.98
  758.9 11.1 collective-permute-start.102
  780.7 10.8 collective-permute-start.106
  802.7 11.3 %collective-permute-start.110 = (f32[10,34,1]{2,1,0:T(8,128)S(1)}, f32[10,34,1]{2,1,0:T(8,128)S(1)}, u32[]{:S(2)}, u32[]{:S(2)}) collective-permute-start(f32[10,34,1]{2,1,0:T(8,128)S(1)} %get-tuple-element.31), channel_id=1, source_target_pairs={{1,0},{2,1},{3,2},{4,3},{5,4},{6,5},{7,6},{8,7},{9,8},{10,9},{11,1... | collective-permute-start | bytes 4088 | tf_op jit(solution)/shard_map/ppermute | solution.py:20
  824.4 10.8 collective-permute-start.114
  846.0 10.8 collective-permute-start.118
  867.5 10.8 collective-permute-start.122
  985.6 5.6 collective-permute-start.125
  995.0 8.6 collective-permute-start.126
  998.9 5.8 collective-permute-start.127
  1012.8 10.0 collective-permute-start.130
  1033.5 10.8 collective-permute-start.134
  1055.0 10.8 collective-permute-start.138
  1076.5 10.9 collective-permute-start.142
  1098.1 11.1 collective-permute-start.146
  (104 other events, 537.5 us)
where the time goes:
time: 1120 us; the launch traced here: 1110 us
  starting transfers between devices  595 us (53%)
  blocking collectives  305 us (27%)
  waiting for transfers between devices  180 us (16%)
  other arithmetic  17.6 us (2%)
    ppermute x74, starting transfers between devices, extended(): lax.ppermute(lax.slice_in_dim(block, 0, width, axis=dim), axis, backward)  404 us
    psum x2, blocking collectives, squares(): return lax.psum(jnp.sum(residual * residual), ('lat', 'lon'))  203 us
    ppermute x74, starting transfers between devices, extended(): lax.ppermute(lax.slice_in_dim(block, block.shape[dim] - width, None, axis...  191 us
    ppermute x74, waiting for transfers between devices, extended(): lax.ppermute(lax.slice_in_dim(block, block.shape[dim] - width, None, axis...  176 us
    psum x1, blocking collectives, per_device(): alpha = norm_now / lax.psum(jnp.sum(direction * image), ('lat', 'lon'))  102 us
  transfers between devices with their start and end apart: 148, of which 74 were waited for; matrix products, arithmetic and copies ran while one was open for 0% of the time, Pallas kernels for 0%

commit v1 on v0

v1 whole, which is shorter than its diff:
```python
import jax
import jax.numpy as jnp
from jax import lax
from jax.experimental import pallas as pl
from jax.experimental.pallas import tpu as pltpu
from jax.sharding import PartitionSpec as P

NCAT = 5
FIELDS = 10
OBS = 8
STEPS = 6
HALO = 12
EDGE = 16
ROWS = 32
COLS = 128
TALL = ROWS + 2 * EDGE
WIDE = 2 * COLS

VMEM = pl.BlockSpec(memory_space=pltpu.VMEM)
SMEM = pl.BlockSpec(memory_space=pltpu.SMEM)
PARAMS = pltpu.CompilerParams(vmem_limit_bytes=48 << 20)


def f32(*shape):
    return jax.ShapeDtypeStruct(shape, jnp.float32)


def lanes(rows):
    return lax.broadcasted_iota(jnp.int32, (rows, COLS), 1)


def rounded(values):
    return values.astype(jnp.bfloat16).astype(jnp.float32)


def pack(planes, start):
    lane = lanes(planes[0].shape[0])
    packed = jnp.zeros_like(planes[0])
    for place, plane in enumerate(planes):
        moved = pltpu.roll(plane, (HALO * place - start) % COLS, 1)
        packed = jnp.where(
            (lane >= HALO * place) & (lane < HALO * (place + 1)), moved, packed
        )
    return packed


def spread(weights, vector, f):
    total = weights[f * OBS].astype(jnp.float32) * vector[f * OBS : f * OBS + 1]
    for slot in range(1, OBS):
        at = f * OBS + slot
        total = total + weights[at].astype(jnp.float32) * vector[at : at + 1]
    return total


def observe(weights, totals):
    rows = []
    for f in range(2):
        for slot in range(OBS):
            product = weights[f * OBS + slot].astype(jnp.float32) * totals[f]
            rows.append(jnp.sum(product, axis=0, keepdims=True))
    seen = jnp.sum(jnp.concatenate(rows, axis=0), axis=1, keepdims=True)
    return jnp.broadcast_to(seen, (2 * OBS, COLS))


def strips(planes, odd, out_a, out_b, at):
    left = pack(planes, 0)
    right = pack(planes, COLS - HALO)
    rows = left.shape[0]
    out_a[at : at + rows] = jnp.where(odd, right, left)
    out_b[at : at + rows] = jnp.where(odd, left, right)


def first_kernel(
    odd_ref, count_ref, innovation_ref, precision_ref, diffusivity, mask, weights,
    base, send_a, send_b, start_vector, keep,
):
    ocean = mask[...].astype(jnp.float32)
    odd = odd_ref[0] == 1
    count = count_ref[0, 0]
    for f in range(2):
        for slot in range(OBS):
            at = f * OBS + slot
            kept = jnp.where(slot < count, precision_ref[f, slot], 0.0)
            keep[at : at + 1] = jnp.full((1, COLS), kept, jnp.float32)
            start_vector[at : at + 1] = jnp.full(
                (1, COLS), kept * innovation_ref[f, slot], jnp.float32
            )
    vector = rounded(start_vector[...])
    start_vector[...] = vector
    for k in range(FIELDS):
        base[k] = diffusivity[k] * ocean
    for f in range(2):
        base[FIELDS + f] = ocean * spread(weights, vector, f)
    strips([base[k] for k in range(FIELDS)], odd, send_a, send_b, 0)
    strips([base[FIELDS], base[FIELDS + 1]], odd, send_a, send_b, ROWS)


def widen(main, left, right, place):
    rows = main.shape[0]
    lane = lanes(rows)
    right = pltpu.roll(right, (-HALO * place) % COLS, 1)
    left = pltpu.roll(left, (COLS - HALO - HALO * place) % COLS, 1)
    side = jnp.where(lane < HALO, right, jnp.where(lane >= COLS - HALO, left, 0.0))
    return jnp.concatenate([main, side], axis=1)


def around(field, rows_by, cols_by):
    if rows_by:
        field = pltpu.roll(field, rows_by % field.shape[0], 0)
    if cols_by:
        field = pltpu.roll(field, cols_by % field.shape[1], 1)
    return field


def two_factors(scaled, ocean, ocean_east, ocean_north, field):
    east = 0.5 * (scaled * ocean_east + around(scaled, 0, -1) * ocean)
    north = 0.5 * (scaled * ocean_north + around(scaled, -1, 0) * ocean)
    west = around(east, 0, 1)
    south = around(north, 1, 0)
    middle = 1.0 - east - west - north - south
    faces = [middle, east, west, north, south]

    def step(x, faces):
        middle, east, west, north, south = faces
        return (
            middle * x
            + (east * around(x, 0, -1) + west * around(x, 0, 1))
            + (north * around(x, -1, 0) + south * around(x, 1, 0))
        )

    x = field
    for _ in range(4):
        x = step(x, faces)
    cut = EDGE - 8
    x = x[cut:-cut]
    faces = [face[cut:-cut] for face in faces]
    for _ in range(4, STEPS):
        x = step(x, faces)
    first = x[8:-8, :COLS]
    x = x * ocean[cut:-cut]
    for _ in range(STEPS):
        x = step(x, faces)
    return first, x[8:-8, :COLS] * ocean[EDGE:-EDGE, :COLS]


def sweep(scaled, oceans, fields, weights, out_x, out_y, totals):
    totals[...] = jnp.zeros_like(totals)

    def one(category, carry):
        for f in range(2):
            k = f * NCAT + category
            first, second = two_factors(
                scaled[k], oceans[0], oceans[1], oceans[2], fields[f]
            )
            out_x[k] = first
            out_y[k] = second
            totals[f] = totals[f] + second
        return carry

    lax.fori_loop(0, NCAT, one, 0)
    return observe(weights, totals)


def sided(odd, a, b):
    return jnp.where(odd, b, a), jnp.where(odd, a, b)


def second_kernel(
    odd_ref, base, got_a, got_b, above, below, weights, start_vector, keep,
    out_x, out_y, scaled, oceans, spread_out, send_a, send_b, vectors,
    fields, totals,
):
    odd = odd_ref[0] == 1
    planes = FIELDS + 2
    halves = []
    for half in range(2):
        pair = []
        for side, got in enumerate((got_a, got_b)):
            at = planes * EDGE + (2 * side + half) * EDGE
            pair.append(
                jnp.concatenate(
                    [above[at : at + EDGE], got[half * ROWS : (half + 1) * ROWS], below[at : at + EDGE]],
                    axis=0,
                )
            )
        halves.append(sided(odd, *pair))

    def whole(k, left, right, place):
        at = k * EDGE
        main = jnp.concatenate([above[at : at + EDGE], base[k], below[at : at + EDGE]], axis=0)
        return widen(main, left, right, place)

    for k in range(FIELDS):
        scaled[k] = whole(k, *halves[0], k)
    for f in range(2):
        fields[f] = whole(FIELDS + f, *halves[1], f)
    ocean = jnp.where(scaled[0] > 0.0, 1.0, 0.0)
    oceans[0] = ocean
    oceans[1] = around(ocean, 0, -1)
    oceans[2] = around(ocean, -1, 0)
    seen = sweep(scaled, oceans, fields, weights, out_x, out_y, totals)
    vector = rounded(keep[...] * seen)
    vectors[0] = seen
    vectors[1] = vector
    own = oceans[0, EDGE:-EDGE, :COLS]
    for f in range(2):
        spread_out[f] = own * spread(weights, vector, f)
    strips([spread_out[0], spread_out[1]], odd, send_a, send_b, 0)


def third_kernel(
    odd_ref, spread_in, got_a, got_b, above, below, weights, start_vector, keep,
    scaled, oceans, vectors,
    out_x, out_y, sums,
    fields, totals,
):
    odd = odd_ref[0] == 1
    pair = []
    for side, got in enumerate((got_a, got_b)):
        at = (2 + side) * EDGE
        pair.append(jnp.concatenate([above[at : at + EDGE], got[...], below[at : at + EDGE]], axis=0))
    left, right = sided(odd, *pair)
    for f in range(2):
        at = f * EDGE
        main = jnp.concatenate([above[at : at + EDGE], spread_in[f], below[at : at + EDGE]], axis=0)
        fields[f] = widen(main, left, right, f)
    later = sweep(scaled, oceans, fields, weights, out_x, out_y, totals)
    seen = vectors[0]
    vector = vectors[1]
    start = start_vector[...]
    kept = keep[...]
    terms = [
        start * seen, vector * seen, vector * later,
        seen * kept * seen, seen * kept * later, later * kept * later,
    ]
    lane = lanes(1)
    row = jnp.zeros((1, COLS), jnp.float32)
    for place, term in enumerate(terms):
        row = jnp.where(lane == place, jnp.sum(term, axis=0, keepdims=True), row)
    sums[...] = jnp.broadcast_to(row, sums.shape)


def last_kernel(sums, x_first, y_first, x_second, y_second, control, increment):
    row = jnp.sum(sums[...], axis=0, keepdims=True)
    lane = lanes(1)
    a, b, c, k00, k01, k11 = [
        jnp.sum(jnp.where(lane == place, row, 0.0), axis=1, keepdims=True) for place in range(6)
    ]
    b, c, k00, k01, k11 = [value / a for value in (b, c, k00, k01, k11)]
    alpha = 1.0 / (1.0 + b)
    beta = (c - b * b) * alpha * alpha
    share = 1.0 - alpha + beta
    below = (share * share * (1.0 + k00)) - 2.0 * share * alpha * (b + k01) + alpha * alpha * (c + k11)
    later = beta / below
    first = jnp.broadcast_to(alpha + later * share, (ROWS, COLS))
    second = jnp.broadcast_to(-later * alpha, (ROWS, COLS))
    for k in range(FIELDS):
        control[k] = first * x_first[k] + second * x_second[k]
        increment[k] = first * y_first[k] + second * y_second[k]


def per_device(diffusivity, land_mask, obs_weights, innovation, precision_weights, obs_count):
    lat_count = lax.axis_size("lat")
    lon_count = lax.axis_size("lon")
    odd = (lax.axis_index("lon") % 2).astype(jnp.int32).reshape(1)
    down = [(i, i + 1) for i in range(lat_count - 1)]
    up = [(i + 1, i) for i in range(lat_count - 1)]
    within = [(i, i ^ 1) for i in range(lon_count)]
    between = [(i, (i + 1 if i % 2 else i - 1) % lon_count) for i in range(lon_count)]
    weights = obs_weights.reshape(2 * OBS, ROWS, COLS)

    base, send_a, send_b, start_vector, keep = pl.pallas_call(
        first_kernel,
        out_shape=(f32(FIELDS + 2, ROWS, COLS), f32(2 * ROWS, COLS), f32(2 * ROWS, COLS),
                   f32(2 * OBS, COLS), f32(2 * OBS, COLS)),
        in_specs=[SMEM] * 4 + [VMEM] * 3,
        out_specs=[VMEM] * 5,
        compiler_params=PARAMS,
        name="first",
    )(odd, obs_count, innovation.reshape(2, OBS), precision_weights.reshape(2, OBS),
      diffusivity, land_mask, weights)

    def exchange(planes, send_a, send_b):
        got_a = lax.ppermute(send_a, "lon", between)
        got_b = lax.ppermute(send_b, "lon", within)
        halves = send_a.shape[0] // ROWS

        def edge(at):
            parts = [planes[:, at : at + EDGE].reshape(-1, COLS)]
            for got in (got_a, got_b):
                for half in range(halves):
                    parts.append(got[half * ROWS + at : half * ROWS + at + EDGE])
            return jnp.concatenate(parts, axis=0)

        above = lax.ppermute(edge(ROWS - EDGE), "lat", down)
        below = lax.ppermute(edge(0), "lat", up)
        return got_a, got_b, above, below

    x_first, y_first, scaled, oceans, spread_first, send_a, send_b, vectors = pl.pallas_call(
        second_kernel,
        out_shape=(f32(FIELDS, ROWS, COLS), f32(FIELDS, ROWS, COLS), f32(FIELDS, TALL, WIDE),
                   f32(3, TALL, WIDE), f32(2, ROWS, COLS), f32(ROWS, COLS), f32(ROWS, COLS),
                   f32(2, 2 * OBS, COLS)),
        in_specs=[SMEM] + [VMEM] * 8,
        out_specs=[VMEM] * 8,
        scratch_shapes=[pltpu.VMEM((2, TALL, WIDE), jnp.float32),
                        pltpu.VMEM((2, ROWS, COLS), jnp.float32)],
        compiler_params=PARAMS,
        name="second",
    )(odd, base, *exchange(base, send_a, send_b), weights, start_vector, keep)

    x_second, y_second, sums = pl.pallas_call(
        third_kernel,
        out_shape=(f32(FIELDS, ROWS, COLS), f32(FIELDS, ROWS, COLS), f32(lon_count, COLS)),
        in_specs=[SMEM] + [VMEM] * 11,
        out_specs=[VMEM] * 3,
        scratch_shapes=[pltpu.VMEM((2, TALL, WIDE), jnp.float32),
                        pltpu.VMEM((2, ROWS, COLS), jnp.float32)],
        compiler_params=PARAMS,
        name="third",
    )(odd, spread_first, *exchange(spread_first, send_a, send_b), weights, start_vector, keep,
      scaled, oceans, vectors)

    sums = lax.all_to_all(sums, "lon", 0, 0, tiled=True)
    sums = jnp.broadcast_to(jnp.sum(sums, axis=0, keepdims=True), (lat_count, COLS))
    sums = lax.all_to_all(sums, "lat", 0, 0, tiled=True)
    return pl.pallas_call(
        last_kernel,
        out_shape=(f32(FIELDS, ROWS, COLS), f32(FIELDS, ROWS, COLS)),
        in_specs=[VMEM] * 5,
        out_specs=[VMEM] * 2,
        compiler_params=PARAMS,
        name="last",
    )(sums, x_first, y_first, x_second, y_second)


def solution(mesh):
    return jax.shard_map(
        per_device,
        mesh=mesh,
        in_specs=(
            P(None, "lat", "lon"),
            P("lat", "lon"),
            P(None, None, "lat", "lon"),
            P(None, "lat", "lon", None),
            P(None, "lat", "lon", None),
            P("lat", "lon"),
        ),
        out_specs=(P(None, "lat", "lon"), P(None, "lat", "lon")),
        check_vma=False,
    )
```

time: 1120 us -> 96.5 us (0.09)
  starting transfers between devices: 595 us -> 31.1 us
  blocking collectives: 305 us -> 38.5 us
  waiting for transfers between devices: 180 us -> 6.81 us
  other arithmetic: 17.6 us -> 0.06 us
  Pallas kernels: 0 us -> 15.4 us
    ppermute x148 -> x8, starting transfers between devices: 595 us -> 31.1 us  [the longest x2 13.9 us: exchange(): got_b = lax.ppermute(send_b, 'lon', within)]
    psum x3 -> x0, blocking collectives: 305 us -> none  [the longest x2 203 us: squares(): return lax.psum(jnp.sum(residual * residual), ('lat', 'lon'))]
    ppermute x148 -> x8, waiting for transfers between devices: 180 us -> 6.81 us  [the longest x2 3.76 us: exchange(): below = lax.ppermute(edge(0), 'lat', up)]
    all_to_all x0 -> x2, blocking collectives: none -> 38.5 us  [the longest x1 24.3 us: per_device(): sums = lax.all_to_all(sums, 'lat', 0, 0, tiled=True)]
    pallas_call x0 -> x4, Pallas kernels: none -> 15.4 us  [the longest x1 7.07 us: per_device(): pl.pallas_call(second_kernel, out_shape=(f32(FIELDS, ROWS, COLS), f32(FIE...]
  transfers between devices with their start and end apart: 148 -> 8, of which waited for: 74 -> 5; matrix products, arithmetic and copies ran while one was open for 0% -> 0% of each run, Pallas kernels for 0% -> 0%
where the time goes in v1:
time: 96.5 us; the launch traced here: 95.9 us
  blocking collectives  38.5 us (40%)
  starting transfers between devices  31.1 us (32%)
  Pallas kernels  15.4 us (16%)
  waiting for transfers between devices  6.81 us (7%)
  local copies, waits for them, and re-layouts  2.57 us (3%)
  between operations  1.5 us (2%)
    all_to_all x1, blocking collectives, per_device(): sums = lax.all_to_all(sums, 'lat', 0, 0, tiled=True)  24.3 us
    all_to_all x1, blocking collectives, per_device(): sums = lax.all_to_all(sums, 'lon', 0, 0, tiled=True)  14.2 us
    ppermute x2, starting transfers between devices, exchange(): got_b = lax.ppermute(send_b, 'lon', within)  13.9 us
    ppermute x2, starting transfers between devices, exchange(): above = lax.ppermute(edge(ROWS - EDGE), 'lat', down)  8.09 us
    pallas_call x1, Pallas kernels, per_device(): pl.pallas_call(second_kernel, out_shape=(f32(FIELDS, ROWS, COLS), f32(FIE...  7.07 us
    pallas_call x1, Pallas kernels, per_device(): pl.pallas_call(third_kernel, out_shape=(f32(FIELDS, ROWS, COLS), f32(FIEL...  6.78 us
    ppermute x2, starting transfers between devices, exchange(): got_a = lax.ppermute(send_a, 'lon', between)  6.52 us
    ppermute x2, waiting for transfers between devices, exchange(): below = lax.ppermute(edge(0), 'lat', up)  3.76 us
  transfers between devices with their start and end apart: 8, of which 5 were waited for; matrix products, arithmetic and copies ran while one was open for 0% of the time, Pallas kernels for 0%

profile of v1, /device:TPU:1, one launch (start us, length us, event | category | flops | bytes accessed | tf_op | source)
XLA Modules:
  0.0 95.9 jit_solution(12905238178044357669)
XLA Ops:
  0.6 0.0 copy-start.3
  1.3 0.0 copy-start.5
  1.3 0.0 copy-start.4
  1.3 0.0 copy-done.3
  1.4 0.6 copy-done.5
  2.0 0.0 copy-done.4
  2.0 0.0 copy-start
  2.0 0.9 copy-done
  2.9 0.0 copy-start.2
  2.9 0.9 copy-done.2
  3.8 0.7 first.1
  4.6 4.6 %collective-permute-start = (f32[64,128]{1,0:T(8,128)S(1)}, f32[64,128]{1,0:T(8,128)S(1)}, u32[]{:S(2)}, u32[]{:S(2)}) collective-permute-start(f32[64,128]{1,0:T(8,128)S(1)} %get-tuple-element.19), channel_id=1, source_target_pairs={{0,31},{1,2},{2,1},{3,4},{4,3},{5,6},{6,5},{7,8},{8,7},{9,10},{10,... | collective-permute-start | bytes 98312 | tf_op jit(solution)/shard_map/ppermute | solution.py:284
  9.2 6.1 %collective-permute-start.1 = (f32[64,128]{1,0:T(8,128)S(1)}, f32[64,128]{1,0:T(8,128)S(1)}, u32[]{:S(2)}, u32[]{:S(2)}) collective-permute-start(f32[64,128]{1,0:T(8,128)S(1)} %get-tuple-element.20), channel_id=1, source_target_pairs={{0,1},{1,0},{2,3},{3,2},{4,5},{5,4},{6,7},{7,6},{8,9},{9,8},{10,11... | collective-permute-start | bytes 98312 | tf_op jit(solution)/shard_map/ppermute | solution.py:285
  15.3 0.0 copy-start.1
  15.3 0.0 collective-permute-done.got_a
  15.4 0.7 collective-permute-done.1.got_b
  16.1 1.3 %collective-permute-start.3 = (f32[256,128]{1,0:T(8,128)S(1)}, f32[256,128]{1,0:T(8,128)S(1)}, u32[]{:S(2)}, u32[]{:S(2)}) collective-permute-start(f32[256,128]{1,0:T(8,128)S(1)} %get-tuple-element.38), channel_id=1, source_target_pairs={{32,0},{64,32},{96,64},{128,96},{160,128},{192,160},{224,192},{256... | collective-permute-start | bytes 393224 | tf_op jit(solution)/shard_map/ppermute | solution.py:296
  17.4 4.0 %collective-permute-start.2 = (f32[256,128]{1,0:T(8,128)S(1)}, f32[256,128]{1,0:T(8,128)S(1)}, u32[]{:S(2)}, u32[]{:S(2)}) collective-permute-start(f32[256,128]{1,0:T(8,128)S(1)} %get-tuple-element.39), channel_id=1, source_target_pairs={{0,32},{32,64},{64,96},{96,128},{128,160},{160,192},{192,224},{224... | collective-permute-start | bytes 393224 | tf_op jit(solution)/shard_map/ppermute | solution.py:295
  21.4 0.4 collective-permute-done.3.below
  21.8 1.5 %collective-permute-done.2.above = f32[256,128]{1,0:T(8,128)S(1)} collective-permute-done((f32[256,128]{1,0:T(8,128)S(1)}, f32[256,128]{1,0:T(8,128)S(1)}, u32[]{:S(2)}, u32[]{:S(2)}) %collective-permute-start.2) | collective-permute-done | bytes 131104 | tf_op jit(solution)/shard_map/ppermute | solution.py:295
  23.3 0.0 copy-done.1
  23.3 7.1 %second.1 = (f32[10,32,128]{2,1,0:T(8,128)S(1)}, f32[10,32,128]{2,1,0:T(8,128)S(1)}, f32[10,64,256]{2,1,0:T(8,128)S(1)}, f32[3,64,256]{2,1,0:T(8,128)S(1)}, f32[...) custom-call(s32[1]{0:T(128)} %bitcast.odd_ref, ...), custom_call_target="tpu_custom_call" | custom-call | tf_op jit(solution)/shard_map/second/pallas_call | solution.py:299
  30.4 1.9 %collective-permute-start.4 = (f32[32,128]{1,0:T(8,128)S(1)}, f32[32,128]{1,0:T(8,128)S(1)}, u32[]{:S(2)}, u32[]{:S(2)}) collective-permute-start(f32[32,128]{1,0:T(8,128)S(1)} %get-tuple-element.24), channel_id=1, source_target_pairs={{0,31},{1,2},{2,1},{3,4},{4,3},{5,6},{6,5},{7,8},{8,7},{9,10},{10,... | collective-permute-start | bytes 49160 | tf_op jit(solution)/shard_map/ppermute | solution.py:284
  32.3 7.8 %collective-permute-start.5 = (f32[32,128]{1,0:T(8,128)S(1)}, f32[32,128]{1,0:T(8,128)S(1)}, u32[]{:S(2)}, u32[]{:S(2)}) collective-permute-start(f32[32,128]{1,0:T(8,128)S(1)} %get-tuple-element.25), channel_id=1, source_target_pairs={{0,1},{1,0},{2,3},{3,2},{4,5},{5,4},{6,7},{7,6},{8,9},{9,8},{10,11... | collective-permute-start | bytes 49160 | tf_op jit(solution)/shard_map/ppermute | solution.py:285
  40.1 0.0 collective-permute-done.4.got_a
  40.2 0.8 collective-permute-done.5.got_b
  41.0 4.1 %collective-permute-start.6 = (f32[64,128]{1,0:T(8,128)S(1)}, f32[64,128]{1,0:T(8,128)S(1)}, u32[]{:S(2)}, u32[]{:S(2)}) collective-permute-start(f32[64,128]{1,0:T(8,128)S(1)} %pad_maximum_fusion), channel_id=1, source_target_pairs={{0,32},{32,64},{64,96},{96,128},{128,160},{160,192},{192,224},{224... | collective-permute-start | bytes 98312 | tf_op jit(solution)/shard_map/ppermute | solution.py:295
  45.1 1.3 %collective-permute-start.7 = (f32[64,128]{1,0:T(8,128)S(1)}, f32[64,128]{1,0:T(8,128)S(1)}, u32[]{:S(2)}, u32[]{:S(2)}) collective-permute-start(f32[64,128]{1,0:T(8,128)S(1)} %pad_maximum_fusion.1), channel_id=1, source_target_pairs={{32,0},{64,32},{96,64},{128,96},{160,128},{192,160},{224,192},{256... | collective-permute-start | bytes 98312 | tf_op jit(solution)/shard_map/ppermute | solution.py:296
  46.4 0.0 collective-permute-done.6.above
  46.4 3.3 %collective-permute-done.7.below = f32[64,128]{1,0:T(8,128)S(1)} collective-permute-done((f32[64,128]{1,0:T(8,128)S(1)}, f32[64,128]{1,0:T(8,128)S(1)}, u32[]{:S(2)}, u32[]{:S(2)}) %collective-permute-start.7) | collective-permute-done | bytes 32800 | tf_op jit(solution)/shard_map/ppermute | solution.py:296
  49.7 6.8 %third.1 = (f32[10,32,128]{2,1,0:T(8,128)S(1)}, f32[10,32,128]{2,1,0:T(8,128)S(1)}, f32[32,128]{1,0:T(8,128)S(1)}) custom-call(s32[1]{0:T(128)} %bitcast.odd_ref, f32[2,32,128]{2,1,0:T(8,128)S(1)} %get-tuple-element.23.spread_in, f32[32,128]{1,0:T(8,128)S(1)} %collective-permute-done.4.got_a, f32[32,128]{1,0:T(8,128)S(1)} %collective-permute-done.5.got_b, ...), custom_call_target="tpu_custom_call" | custom-call | tf_op jit(solution)/shard_map/third/pallas_call | solution.py:312
  56.5 14.2 %all_to_all.17 = f32[32,1,128]{2,1,0:T(1,128)S(1)} all-to-all(f32[32,1,128]{2,1,0:T(1,128)S(1)} %bitcast.16), channel_id=1, replica_groups=mesh['lat'=16,'lon'=32] {'lon'}, dimensions={0} | all-to-all | bytes 32768 | tf_op jit(solution)/shard_map/all_to_all | solution.py:324
  70.7 0.1 reduce_sum.9
  70.8 24.3 %all_to_all.18 = f32[16,1,128]{2,1,0:T(1,128)S(1)} all-to-all(f32[16,1,128]{2,1,0:T(1,128)S(1)} %broadcast_in_dim.2), channel_id=1, replica_groups=mesh['lat'=16,'lon'=32] {'lat'}, dimensions={0} | all-to-all | bytes 16384 | tf_op jit(solution)/shard_map/all_to_all | solution.py:326
  95.1 0.9 last.1
  (12 shorter events, 0.1 us)
Async XLA Ops:
  0.6 0.7 copy-start.3
  1.3 0.7 copy-start.5
  1.3 0.7 copy-start.4
  2.0 0.9 copy-start
  2.9 0.9 copy-start.2
  4.6 10.8 %collective-permute-start = (f32[64,128]{1,0:T(8,128)S(1)}, f32[64,128]{1,0:T(8,128)S(1)}, u32[]{:S(2)}, u32[]{:S(2)}) collective-permute-start(f32[64,128]{1,0:T(8,128)S(1)} %get-tuple-element.19), channel_id=1, source_target_pairs={{0,31},{1,2},{2,1},{3,4},{4,3},{5,6},{6,5},{7,8},{8,7},{9,10},{10,... | collective-permute-start | bytes 98312 | tf_op jit(solution)/shard_map/ppermute | solution.py:284
  9.2 7.0 %collective-permute-start.1 = (f32[64,128]{1,0:T(8,128)S(1)}, f32[64,128]{1,0:T(8,128)S(1)}, u32[]{:S(2)}, u32[]{:S(2)}) collective-permute-start(f32[64,128]{1,0:T(8,128)S(1)} %get-tuple-element.20), channel_id=1, source_target_pairs={{0,1},{1,0},{2,3},{3,2},{4,5},{5,4},{6,7},{7,6},{8,9},{9,8},{10,11... | collective-permute-start | bytes 98312 | tf_op jit(solution)/shard_map/ppermute | solution.py:285
  15.3 8.0 %copy-start.1 = (bf16[2,8,32,128]{3,2,1,0:T(8,128)(2,1)S(1)}, bf16[2,8,32,128]{3,2,1,0:T(8,128)(2,1)}, u32[]{:S(2)}) copy-start(bf16[2,8,32,128]{3,2,1,0:T(8,128)(2,1)} %param.8) | copy-start | bytes 393220
  16.1 5.7 %collective-permute-start.3 = (f32[256,128]{1,0:T(8,128)S(1)}, f32[256,128]{1,0:T(8,128)S(1)}, u32[]{:S(2)}, u32[]{:S(2)}) collective-permute-start(f32[256,128]{1,0:T(8,128)S(1)} %get-tuple-element.38), channel_id=1, source_target_pairs={{32,0},{64,32},{96,64},{128,96},{160,128},{192,160},{224,192},{256... | collective-permute-start | bytes 393224 | tf_op jit(solution)/shard_map/ppermute | solution.py:296
  17.4 5.9 %collective-permute-start.2 = (f32[256,128]{1,0:T(8,128)S(1)}, f32[256,128]{1,0:T(8,128)S(1)}, u32[]{:S(2)}, u32[]{:S(2)}) collective-permute-start(f32[256,128]{1,0:T(8,128)S(1)} %get-tuple-element.39), channel_id=1, source_target_pairs={{0,32},{32,64},{64,96},{96,128},{128,160},{160,192},{192,224},{224... | collective-permute-start | bytes 393224 | tf_op jit(solution)/shard_map/ppermute | solution.py:295
  30.4 9.7 %collective-permute-start.4 = (f32[32,128]{1,0:T(8,128)S(1)}, f32[32,128]{1,0:T(8,128)S(1)}, u32[]{:S(2)}, u32[]{:S(2)}) collective-permute-start(f32[32,128]{1,0:T(8,128)S(1)} %get-tuple-element.24), channel_id=1, source_target_pairs={{0,31},{1,2},{2,1},{3,4},{4,3},{5,6},{6,5},{7,8},{8,7},{9,10},{10,... | collective-permute-start | bytes 49160 | tf_op jit(solution)/shard_map/ppermute | solution.py:284
  32.3 8.6 %collective-permute-start.5 = (f32[32,128]{1,0:T(8,128)S(1)}, f32[32,128]{1,0:T(8,128)S(1)}, u32[]{:S(2)}, u32[]{:S(2)}) collective-permute-start(f32[32,128]{1,0:T(8,128)S(1)} %get-tuple-element.25), channel_id=1, source_target_pairs={{0,1},{1,0},{2,3},{3,2},{4,5},{5,4},{6,7},{7,6},{8,9},{9,8},{10,11... | collective-permute-start | bytes 49160 | tf_op jit(solution)/shard_map/ppermute | solution.py:285
  41.0 5.4 %collective-permute-start.6 = (f32[64,128]{1,0:T(8,128)S(1)}, f32[64,128]{1,0:T(8,128)S(1)}, u32[]{:S(2)}, u32[]{:S(2)}) collective-permute-start(f32[64,128]{1,0:T(8,128)S(1)} %pad_maximum_fusion), channel_id=1, source_target_pairs={{0,32},{32,64},{64,96},{96,128},{128,160},{160,192},{192,224},{224... | collective-permute-start | bytes 98312 | tf_op jit(solution)/shard_map/ppermute | solution.py:295
  45.1 4.7 %collective-permute-start.7 = (f32[64,128]{1,0:T(8,128)S(1)}, f32[64,128]{1,0:T(8,128)S(1)}, u32[]{:S(2)}, u32[]{:S(2)}) collective-permute-start(f32[64,128]{1,0:T(8,128)S(1)} %pad_maximum_fusion.1), channel_id=1, source_target_pairs={{32,0},{64,32},{96,64},{128,96},{160,128},{192,160},{224,192},{256... | collective-permute-start | bytes 98312 | tf_op jit(solution)/shard_map/ppermute | solution.py:296

commit v2 on v1

v2 whole, which is shorter than its diff:
```python
import jax
import jax.numpy as jnp
from jax import lax
from jax.experimental import pallas as pl
from jax.experimental.pallas import tpu as pltpu
from jax.sharding import PartitionSpec as P

NCAT = 5
FIELDS = 10
OBS = 8
STEPS = 6
HALO = 12
EDGE = 16
ROWS = 32
COLS = 128
TALL = ROWS + 2 * EDGE
TILES = 7
DEEP = 8 * TILES
GROUP = NCAT + 1
ALL = 2 * GROUP
SLOT = 2 * HALO
PACKS = 3

VMEM = pl.BlockSpec(memory_space=pltpu.VMEM)
ANY = pl.BlockSpec(memory_space=pl.ANY)
PARAMS = pltpu.CompilerParams(vmem_limit_bytes=40 << 20)


def f32(*shape):
    return jax.ShapeDtypeStruct(shape, jnp.float32)


def lanes(rows):
    return lax.broadcasted_iota(jnp.int32, (rows, COLS), 1)


def rounded(values):
    return values.astype(jnp.bfloat16).astype(jnp.float32)


def turn(plane, amount):
    amount = amount % COLS
    return plane if amount == 0 else pltpu.roll(plane, amount, 1)


def spread(weights, vector, f):
    total = weights[f * OBS].astype(jnp.float32) * vector[f * OBS : f * OBS + 1]
    for slot in range(1, OBS):
        at = f * OBS + slot
        total = total + weights[at].astype(jnp.float32) * vector[at : at + 1]
    return total


def observe(weights, totals):
    rows = []
    for f in range(2):
        for slot in range(OBS):
            product = weights[f * OBS + slot].astype(jnp.float32) * totals[f]
            rows.append(jnp.sum(product, axis=0, keepdims=True))
    seen = jnp.sum(jnp.concatenate(rows, axis=0), axis=1, keepdims=True)
    return jnp.broadcast_to(seen, (2 * OBS, COLS))


def strips(odd, planes, out_a, out_b, at):
    lane = lanes(ROWS)
    left = jnp.zeros((ROWS, COLS), jnp.float32)
    right = left
    for place, plane in enumerate(planes):
        start = SLOT * place
        left = jnp.where((lane >= start) & (lane < start + HALO), plane, left)
        right = jnp.where((lane >= start + HALO) & (lane < start + SLOT), plane, right)
    out_a[at : at + ROWS] = jnp.where(odd, left, right)
    out_b[at : at + ROWS] = jnp.where(odd, right, left)


def first_kernel(
    odd_ref, diffusivity_any, mask_any, weights_any, innovation_any, precision_any, count_any,
    base, send_a, send_b, start_vector, keep,
    diffusivity, mask, weights, innovation, precision, count, sems,
):
    pairs = (
        (innovation_any, innovation), (precision_any, precision), (count_any, count),
        (weights_any, weights), (mask_any, mask), (diffusivity_any, diffusivity),
    )
    copies = [
        pltpu.make_async_copy(source, target, sems.at[place])
        for place, (source, target) in enumerate(pairs)
    ]
    for copy in copies:
        copy.start()
    odd = odd_ref[0] == 1
    for copy in copies[:3]:
        copy.wait()
    valid = count[0, 0]
    for f in range(2):
        for slot in range(OBS):
            at = f * OBS + slot
            kept = jnp.where(slot < valid, precision[f, 0, 0, slot], 0.0)
            keep[at : at + 1] = jnp.full((1, COLS), kept, jnp.float32)
            start_vector[at : at + 1] = jnp.full(
                (1, COLS), kept * innovation[f, 0, 0, slot], jnp.float32
            )
    vector = rounded(start_vector[...])
    start_vector[...] = vector
    copies[3].wait()
    copies[4].wait()
    ocean = mask[...].astype(jnp.float32)
    for f in range(2):
        base[FIELDS + f] = turn(ocean * spread(weights, vector, f), HALO + SLOT * f)
    copies[5].wait()
    for k in range(FIELDS):
        base[k] = turn(diffusivity[k] * ocean, HALO + SLOT * (k % NCAT))
    for f in range(2):
        strips(odd, [base[f * NCAT + c] for c in range(NCAT)], send_a, send_b, f * ROWS)
    strips(odd, [base[FIELDS], base[FIELDS + 1]], send_a, send_b, 2 * ROWS)


def tile(t):
    return slice(8 * t, 8 * t + 8)


def deal(natural, plane):
    parts = [natural[plane, pl.ds(EDGE - HALO + t, 8, stride=TILES), :] for t in range(TILES)]
    return jnp.concatenate(parts, axis=0)


def gather_rows(natural, plane, target):
    for t in range(TILES):
        natural[plane, pl.ds(EDGE - HALO + t, 8, stride=TILES), :] = target[tile(t)]


def pick(lane, places, options, other):
    for place, option in zip(places, options):
        other = jnp.where(lane == place, option, other)
    return other


def east_of(planes, lane):
    turned = [pltpu.roll(plane, COLS - 1, 1) for plane in planes]
    last = [HALO + SLOT * c - 1 for c in range(NCAT)]
    mains = [jnp.where(lane == last[c], turned[NCAT], turned[c]) for c in range(NCAT)]
    return mains + [pick(lane, last, turned[:NCAT], turned[NCAT])]


def west_of(planes, lane):
    turned = [pltpu.roll(plane, 1, 1) for plane in planes]
    head = [HALO + SLOT * c for c in range(NCAT)]
    mains = [jnp.where(lane == head[c], turned[NCAT], turned[c]) for c in range(NCAT)]
    return mains + [pick(lane, head, turned[:NCAT], turned[NCAT])]


def north_tile(ref, at, t):
    return ref[at, tile(t + 1)] if t + 1 < TILES else pltpu.roll(ref[at, tile(0)], 7, 0)


def south_tile(ref, at, t):
    return ref[at, tile(t - 1)] if t > 0 else pltpu.roll(ref[at, tile(TILES - 1)], 1, 0)


def make_faces(scaled, faces):
    lane = lanes(8)
    for g in range(2):
        places = [g * GROUP + c for c in range(GROUP)]
        for t in range(TILES):
            here = [scaled[at, tile(t)] for at in places]
            east = [
                jnp.where((x > 0.0) & (y > 0.0), 0.5 * (x + y), 0.0)
                for x, y in zip(here, east_of(here, lane))
            ]
            west = west_of(east, lane)
            for at, x, e, w in zip(places, here, east, west):
                y = north_tile(scaled, at, t)
                faces[1, at, tile(t)] = e
                faces[2, at, tile(t)] = w
                faces[3, at, tile(t)] = jnp.where((x > 0.0) & (y > 0.0), 0.5 * (x + y), 0.0)
        for t in range(TILES):
            for at in places:
                south = south_tile(faces.at[3], at, t)
                faces[4, at, tile(t)] = south
                faces[0, at, tile(t)] = (
                    1.0 - faces[1, at, tile(t)] - faces[2, at, tile(t)]
                ) - (faces[3, at, tile(t)] + south)


def step(source, target, faces):
    lane = lanes(8)
    for t in range(TILES):
        for g in range(2):
            places = [g * GROUP + c for c in range(GROUP)]
            here = [source[at, tile(t)] for at in places]
            east = east_of(here, lane)
            west = west_of(here, lane)
            for at, x, e, w in zip(places, here, east, west):
                along = faces[1, at, tile(t)] * e + faces[2, at, tile(t)] * w
                across = faces[3, at, tile(t)] * north_tile(source, at, t) + faces[
                    4, at, tile(t)
                ] * south_tile(source, at, t)
                target[at, tile(t)] = faces[0, at, tile(t)] * x + (along + across)


def diffuse(field, other, faces):
    def two(_, carry):
        step(field, other, faces)
        step(other, field, faces)
        return carry

    lax.fori_loop(0, STEPS // 2, two, 0)


def sweep(natural, scaled, faces, weights, out_x, out_y, field, other):
    lane = lanes(DEEP)
    pack = deal(natural, 2)
    for f in range(2):
        main = deal(natural, f)
        side = jnp.zeros((DEEP, COLS), jnp.float32)
        for c in range(NCAT):
            field[f * GROUP + c] = turn(main, SLOT * (c - f))
            start = SLOT * c
            side = jnp.where(
                (lane >= start) & (lane < start + SLOT), turn(pack, SLOT * (c - f)), side
            )
        field[f * GROUP + NCAT] = side
    diffuse(field, other, faces)
    for f in range(2):
        for c in range(GROUP):
            at = f * GROUP + c
            if c < NCAT:
                out_x[f * NCAT + c] = field[at]
            field[at] = jnp.where(scaled[at] > 0.0, field[at], 0.0)
    diffuse(field, other, faces)
    totals = []
    for f in range(2):
        total = jnp.zeros((DEEP, COLS), jnp.float32)
        for c in range(NCAT):
            at = f * GROUP + c
            wet = jnp.where(scaled[at] > 0.0, field[at], 0.0)
            out_y[f * NCAT + c] = wet
            total = total + turn(wet, -HALO - SLOT * c)
        gather_rows(natural, f, total)
        totals.append(natural[f, EDGE:-EDGE])
    return observe(weights, totals)


def second_kernel(
    odd_ref, base, got_a, got_b, above, below, weights, start_vector, keep,
    out_x, out_y, scaled, faces, spread_out, send_a, send_b, vectors,
    natural, field, other,
):
    odd = odd_ref[0] == 1
    planes = FIELDS + 2
    strip = planes * EDGE
    for k in range(planes):
        f, c = divmod(k, NCAT)
        at = f * GROUP + c
        natural[at, :EDGE] = above[k * EDGE : (k + 1) * EDGE]
        natural[at, EDGE:-EDGE] = base[k]
        natural[at, -EDGE:] = below[k * EDGE : (k + 1) * EDGE]
    for p in range(PACKS):
        at = NCAT + GROUP * p
        first = strip + p * EDGE
        second = first + PACKS * EDGE
        natural[at, :EDGE] = above[first : first + EDGE] + above[second : second + EDGE]
        natural[at, EDGE:-EDGE] = (
            got_a[p * ROWS : (p + 1) * ROWS] + got_b[p * ROWS : (p + 1) * ROWS]
        )
        natural[at, -EDGE:] = below[first : first + EDGE] + below[second : second + EDGE]
    for at in range(ALL):
        scaled[at] = deal(natural, at)
    make_faces(scaled, faces)
    for place, at in enumerate((2 * GROUP, 2 * GROUP + 1, 2 * GROUP + NCAT)):
        natural[place] = natural[at]
    seen = sweep(natural, scaled, faces, weights, out_x, out_y, field, other)
    vector = rounded(keep[...] * seen)
    vectors[0] = seen
    vectors[1] = vector
    wet = turn(base[0], -HALO) > 0.0
    for f in range(2):
        spread_out[f] = turn(
            jnp.where(wet, spread(weights, vector, f), 0.0), HALO + SLOT * f
        )
    strips(odd, [spread_out[0], spread_out[1]], send_a, send_b, 0)


def third_kernel(
    spread_in, got_a, got_b, above, below, weights, start_vector, keep,
    scaled, faces, vectors,
    out_x, out_y, sums,
    natural, field, other,
):
    for f in range(2):
        natural[f, :EDGE] = above[f * EDGE : (f + 1) * EDGE]
        natural[f, EDGE:-EDGE] = spread_in[f]
        natural[f, -EDGE:] = below[f * EDGE : (f + 1) * EDGE]
    first, second = slice(2 * EDGE, 3 * EDGE), slice(3 * EDGE, 4 * EDGE)
    natural[2, :EDGE] = above[first] + above[second]
    natural[2, EDGE:-EDGE] = got_a[...] + got_b[...]
    natural[2, -EDGE:] = below[first] + below[second]
    later = sweep(natural, scaled, faces, weights, out_x, out_y, field, other)
    seen = vectors[0]
    vector = vectors[1]
    start = start_vector[...]
    kept = keep[...]
    terms = [
        start * seen, vector * seen, vector * later,
        seen * kept * seen, seen * kept * later, later * kept * later,
    ]
    lane = lanes(1)
    row = jnp.zeros((1, COLS), jnp.float32)
    for place, term in enumerate(terms):
        row = jnp.where(lane == place, jnp.sum(term, axis=0, keepdims=True), row)
    sums[...] = jnp.broadcast_to(row, sums.shape)


def last_kernel(sums, x_first, y_first, x_second, y_second, control, increment, natural):
    row = jnp.sum(sums[...], axis=0, keepdims=True)
    lane = lanes(1)
    a, b, c, k00, k01, k11 = [
        jnp.sum(jnp.where(lane == place, row, 0.0), axis=1, keepdims=True) for place in range(6)
    ]
    b, c, k00, k01, k11 = [value / a for value in (b, c, k00, k01, k11)]
    alpha = 1.0 / (1.0 + b)
    beta = (c - b * b) * alpha * alpha
    share = 1.0 - alpha + beta
    below = (share * share * (1.0 + k00)) - 2.0 * share * alpha * (b + k01) + alpha * alpha * (c + k11)
    later = beta / below
    first = jnp.broadcast_to(alpha + later * share, (DEEP, COLS))
    second = jnp.broadcast_to(-later * alpha, (DEEP, COLS))
    for k in range(FIELDS):
        for place, (out, one, two) in enumerate(
            ((control, x_first, x_second), (increment, y_first, y_second))
        ):
            at = 2 * k + place
            gather_rows(natural, at, first * one[k] + second * two[k])
            out[k] = turn(natural[at, EDGE:-EDGE], -HALO - SLOT * (k % NCAT))


def call(kernel, name, outs, ins, scratch):
    return pl.pallas_call(
        kernel, out_shape=outs, in_specs=ins, out_specs=[VMEM] * len(outs),
        scratch_shapes=scratch, compiler_params=PARAMS, name=name,
    )


SMEM = pl.BlockSpec(memory_space=pltpu.SMEM)
SWEEP = [pltpu.VMEM((ALL, DEEP, COLS), jnp.float32)] * 2


def first_call():
    return call(
        first_kernel, "first",
        (f32(FIELDS + 2, ROWS, COLS), f32(PACKS * ROWS, COLS), f32(PACKS * ROWS, COLS),
         f32(2 * OBS, COLS), f32(2 * OBS, COLS)),
        [SMEM] + [ANY] * 6,
        [pltpu.VMEM((FIELDS, ROWS, COLS), jnp.float32), pltpu.VMEM((ROWS, COLS), jnp.int32),
         pltpu.VMEM((2 * OBS, ROWS, COLS), jnp.bfloat16), pltpu.SMEM((2, 1, 1, OBS), jnp.float32),
         pltpu.SMEM((2, 1, 1, OBS), jnp.float32), pltpu.SMEM((1, 1), jnp.int32),
         pltpu.SemaphoreType.DMA((6,))],
    )


def second_call():
    return call(
        second_kernel, "second",
        (f32(FIELDS, DEEP, COLS), f32(FIELDS, DEEP, COLS), f32(ALL, DEEP, COLS),
         f32(5, ALL, DEEP, COLS), f32(2, ROWS, COLS), f32(ROWS, COLS), f32(ROWS, COLS),
         f32(2, 2 * OBS, COLS)),
        [SMEM] + [VMEM] * 8,
        [pltpu.VMEM((ALL + GROUP, TALL, COLS), jnp.float32)] + SWEEP,
    )


def third_call(lon_count):
    return call(
        third_kernel, "third",
        (f32(FIELDS, DEEP, COLS), f32(FIELDS, DEEP, COLS), f32(lon_count, COLS)),
        [VMEM] * 11,
        [pltpu.VMEM((3, TALL, COLS), jnp.float32)] + SWEEP,
    )


def last_call():
    return call(
        last_kernel, "last",
        (f32(FIELDS, ROWS, COLS), f32(FIELDS, ROWS, COLS)),
        [VMEM] * 5,
        [pltpu.VMEM((2 * FIELDS, TALL, COLS), jnp.float32)],
    )


def per_device(diffusivity, land_mask, obs_weights, innovation, precision_weights, obs_count):
    lat_count = lax.axis_size("lat")
    lon_count = lax.axis_size("lon")
    odd = (lax.axis_index("lon") % 2).astype(jnp.int32).reshape(1)
    down = [(i, i + 1) for i in range(lat_count - 1)]
    up = [(i + 1, i) for i in range(lat_count - 1)]
    chips = [[i, i + 1] for i in range(0, lon_count, 2)]
    between = [(i, (i + 1 if i % 2 else i - 1) % lon_count) for i in range(lon_count)]
    weights = obs_weights.reshape(2 * OBS, ROWS, COLS)

    base, send_a, send_b, start_vector, keep = first_call()(
        odd, diffusivity, land_mask, weights, innovation, precision_weights, obs_count
    )

    def exchange(planes, send_a, send_b):
        got_a = lax.ppermute(send_a, "lon", between)
        both = lax.all_gather(send_b, "lon", axis_index_groups=chips)
        got_b = jnp.where(odd[0] == 1, both[0], both[1])
        packs = send_a.shape[0] // ROWS

        def edge(at):
            parts = [planes[:, at : at + EDGE].reshape(-1, COLS)]
            for got in (got_a, got_b):
                for pack in range(packs):
                    parts.append(got[pack * ROWS + at : pack * ROWS + at + EDGE])
            return jnp.concatenate(parts, axis=0)

        above = lax.ppermute(edge(ROWS - EDGE), "lat", down)
        below = lax.ppermute(edge(0), "lat", up)
        return got_a, got_b, above, below

    x_first, y_first, scaled, faces, spread_first, send_a, send_b, vectors = second_call()(
        odd, base, *exchange(base, send_a, send_b), weights, start_vector, keep
    )
    x_second, y_second, sums = third_call(lon_count)(
        spread_first, *exchange(spread_first, send_a, send_b), weights, start_vector, keep,
        scaled, faces, vectors,
    )
    sums = lax.all_to_all(sums, "lon", 0, 0, tiled=True)
    sums = jnp.broadcast_to(jnp.sum(sums, axis=0, keepdims=True), (lat_count, COLS))
    sums = lax.all_to_all(sums, "lat", 0, 0, tiled=True)
    return last_call()(sums, x_first, y_first, x_second, y_second)


def solution(mesh):
    return jax.shard_map(
        per_device,
        mesh=mesh,
        in_specs=(
            P(None, "lat", "lon"),
            P("lat", "lon"),
            P(None, None, "lat", "lon"),
            P(None, "lat", "lon", None),
            P(None, "lat", "lon", None),
            P("lat", "lon"),
        ),
        out_specs=(P(None, "lat", "lon"), P(None, "lat", "lon")),
        check_vma=False,
    )
```

time: 96.5 us -> 91.5 us (0.948)
  blocking collectives: 38.5 us -> 52.8 us
  starting transfers between devices: 31.1 us -> 17.2 us
  Pallas kernels: 15.4 us -> 10.1 us
  waiting for transfers between devices: 6.81 us -> 5.4 us
  local copies, waits for them, and re-layouts: 2.57 us -> 3.96 us
    ppermute x2 -> x0, starting transfers between devices: 13.9 us -> none  [exchange(): got_b = lax.ppermute(send_b, 'lon', within)]
    all_gather x0 -> x2, blocking collectives: none -> 13.5 us  [exchange(): both = lax.all_gather(send_b, 'lon', axis_index_groups=chips)]
    pallas_call x4, Pallas kernels: 15.4 us -> 10.1 us  [the longest x1 4.49 us: per_device(): second_call()]
    all_to_all x1, blocking collectives: 14.2 us -> 16 us  [per_device(): sums = lax.all_to_all(sums, 'lon', 0, 0, tiled=True)]
    ppermute x2 -> x0, waiting for transfers between devices: 1.53 us -> none  [exchange(): got_b = lax.ppermute(send_b, 'lon', within)]
    unnamed x16 -> x18, local copies, waits for them, and re-layouts: 2.53 us -> 3.93 us
    all_to_all x1, blocking collectives: 24.3 us -> 23.2 us  [per_device(): sums = lax.all_to_all(sums, 'lat', 0, 0, tiled=True)]
  transfers between devices with their start and end apart: 8 -> 6, of which waited for: 5 -> 3; matrix products, arithmetic and copies ran while one was open for 0% -> 0% of each run, Pallas kernels for 0% -> 0%
where the time goes in v2:
time: 91.5 us; the launch traced here: 91 us
  blocking collectives  52.8 us (58%)
  starting transfers between devices  17.2 us (19%)
  Pallas kernels  10.1 us (11%)
  waiting for transfers between devices  5.4 us (6%)
  local copies, waits for them, and re-layouts  3.96 us (4%)
  between operations  1.51 us (2%)
    all_to_all x1, blocking collectives, per_device(): sums = lax.all_to_all(sums, 'lat', 0, 0, tiled=True)  23.2 us
    all_to_all x1, blocking collectives, per_device(): sums = lax.all_to_all(sums, 'lon', 0, 0, tiled=True)  16 us
    all_gather x2, blocking collectives, exchange(): both = lax.all_gather(send_b, 'lon', axis_index_groups=chips)  13.5 us
    ppermute x2, starting transfers between devices, exchange(): above = lax.ppermute(edge(ROWS - EDGE), 'lat', down)  8.09 us
    ppermute x2, starting transfers between devices, exchange(): got_a = lax.ppermute(send_a, 'lon', between)  6.52 us
    pallas_call x1, Pallas kernels, per_device(): second_call()  4.49 us
    unnamed x18, local copies, waits for them, and re-layouts  3.93 us
    ppermute x2, waiting for transfers between devices, exchange(): below = lax.ppermute(edge(0), 'lat', up)  3.9 us
  transfers between devices with their start and end apart: 6, of which 3 were waited for; matrix products, arithmetic and copies ran while one was open for 0% of the time, Pallas kernels for 0%

profile of v2, /device:TPU:1, one launch (start us, length us, event | category | flops | bytes accessed | tf_op | source)
XLA Modules:
  0.0 91.0 jit_solution(6157791078328943940)
XLA Ops:
  1.3 0.0 copy-start
  1.3 0.9 copy-done
  2.2 0.0 copy-start.2
  2.2 0.9 %copy-done.2 = f32[10,32,128]{2,1,0:T(8,128)S(1)} copy-done((f32[10,32,128]{2,1,0:T(8,128)S(1)}, f32[10,32,128]{2,1,0:T(8,128)}, u32[]{:S(2)}) %copy-start.2) | copy-done | bytes 163864
  3.1 0.0 copy-start.3
  3.1 0.7 copy-done.3
  3.8 0.0 copy-start.4
  3.8 0.7 copy-done.4
  4.5 0.0 copy-start.5
  4.5 0.7 copy-done.5
  5.2 0.0 copy-start.1
  5.2 0.9 first.1
  6.1 4.6 %collective-permute-start = (f32[96,128]{1,0:T(8,128)S(1)}, f32[96,128]{1,0:T(8,128)S(1)}, u32[]{:S(2)}, u32[]{:S(2)}) collective-permute-start(f32[96,128]{1,0:T(8,128)S(1)} %get-tuple-element.19), channel_id=1, source_target_pairs={{0,31},{1,2},{2,1},{3,4},{4,3},{5,6},{6,5},{7,8},{8,7},{9,10},{10,... | collective-permute-start | bytes 147464 | tf_op jit(solution)/shard_map/ppermute | solution.py:405
  10.7 5.7 %all-gather = f32[192,128]{1,0:T(8,128)S(1)} all-gather(f32[96,128]{1,0:T(8,128)S(1)} %get-tuple-element.20), channel_id=2, replica_groups={{0,1},{2,3},{4,5},{6,7},{8,9},{10,11},{12,13},{14,15},{16,17},{18,19},{..., dimensions={0}, use_global_device_ids=true | all-gather | bytes 147456 | tf_op jit(solution)/shard_map/all_gather | solution.py:406
  16.5 0.0 collective-permute-done.got_a
  16.5 1.3 %collective-permute-start.2 = (f32[288,128]{1,0:T(8,128)S(1)}, f32[288,128]{1,0:T(8,128)S(1)}, u32[]{:S(2)}, u32[]{:S(2)}) collective-permute-start(f32[288,128]{1,0:T(8,128)S(1)} %get-tuple-element.36), channel_id=1, source_target_pairs={{32,0},{64,32},{96,64},{128,96},{160,128},{192,160},{224,192},{256... | collective-permute-start | bytes 442376 | tf_op jit(solution)/shard_map/ppermute | solution.py:418
  17.8 4.0 %collective-permute-start.1 = (f32[288,128]{1,0:T(8,128)S(1)}, f32[288,128]{1,0:T(8,128)S(1)}, u32[]{:S(2)}, u32[]{:S(2)}) collective-permute-start(f32[288,128]{1,0:T(8,128)S(1)} %get-tuple-element.37), channel_id=1, source_target_pairs={{0,32},{32,64},{64,96},{96,128},{128,160},{160,192},{192,224},{224... | collective-permute-start | bytes 442376 | tf_op jit(solution)/shard_map/ppermute | solution.py:417
  21.9 0.6 collective-permute-done.2.below
  22.4 1.5 %collective-permute-done.1.above = f32[288,128]{1,0:T(8,128)S(1)} collective-permute-done((f32[288,128]{1,0:T(8,128)S(1)}, f32[288,128]{1,0:T(8,128)S(1)}, u32[]{:S(2)}, u32[]{:S(2)}) %collective-permute-start.1) | collective-permute-done | bytes 147488 | tf_op jit(solution)/shard_map/ppermute | solution.py:417
  23.9 0.0 copy-done.1
  23.9 4.5 %second.1 = (f32[10,56,128]{2,1,0:T(8,128)S(1)}, f32[10,56,128]{2,1,0:T(8,128)S(1)}, f32[12,56,128]{2,1,0:T(8,128)S(1)}, f32[5,12,56,128]{3,2,1,0:T(8,128)S(1)},...) custom-call(s32[1]{0:T(128)} %bitcast.odd_ref, ...), custom_call_target="tpu_custom_call" | custom-call | tf_op jit(solution)/shard_map/second/pallas_call | solution.py:421
  28.4 1.9 %collective-permute-start.3 = (f32[32,128]{1,0:T(8,128)S(1)}, f32[32,128]{1,0:T(8,128)S(1)}, u32[]{:S(2)}, u32[]{:S(2)}) collective-permute-start(f32[32,128]{1,0:T(8,128)S(1)} %get-tuple-element.24), channel_id=1, source_target_pairs={{0,31},{1,2},{2,1},{3,4},{4,3},{5,6},{6,5},{7,8},{8,7},{9,10},{10,... | collective-permute-start | bytes 49160 | tf_op jit(solution)/shard_map/ppermute | solution.py:405
  30.4 7.8 %all-gather.1 = f32[64,128]{1,0:T(8,128)S(1)} all-gather(f32[32,128]{1,0:T(8,128)S(1)} %get-tuple-element.25), channel_id=3, replica_groups={{0,1},{2,3},{4,5},{6,7},{8,9},{10,11},{12,13},{14,15},{16,17},{18,19},{..., dimensions={0}, use_global_device_ids=true | all-gather | bytes 49152 | tf_op jit(solution)/shard_map/all_gather | solution.py:406
  38.2 0.0 collective-permute-done.3.got_a
  38.2 4.1 %collective-permute-start.4 = (f32[64,128]{1,0:T(8,128)S(1)}, f32[64,128]{1,0:T(8,128)S(1)}, u32[]{:S(2)}, u32[]{:S(2)}) collective-permute-start(f32[64,128]{1,0:T(8,128)S(1)} %pad_maximum_fusion), channel_id=1, source_target_pairs={{0,32},{32,64},{64,96},{96,128},{128,160},{160,192},{192,224},{224... | collective-permute-start | bytes 98312 | tf_op jit(solution)/shard_map/ppermute | solution.py:417
  42.3 1.3 %collective-permute-start.5 = (f32[64,128]{1,0:T(8,128)S(1)}, f32[64,128]{1,0:T(8,128)S(1)}, u32[]{:S(2)}, u32[]{:S(2)}) collective-permute-start(f32[64,128]{1,0:T(8,128)S(1)} %pad_maximum_fusion.1), channel_id=1, source_target_pairs={{32,0},{64,32},{96,64},{128,96},{160,128},{192,160},{224,192},{256... | collective-permute-start | bytes 98312 | tf_op jit(solution)/shard_map/ppermute | solution.py:418
  43.6 0.0 collective-permute-done.4.above
  43.6 3.3 %collective-permute-done.5.below = f32[64,128]{1,0:T(8,128)S(1)} collective-permute-done((f32[64,128]{1,0:T(8,128)S(1)}, f32[64,128]{1,0:T(8,128)S(1)}, u32[]{:S(2)}, u32[]{:S(2)}) %collective-permute-start.5) | collective-permute-done | bytes 32800 | tf_op jit(solution)/shard_map/ppermute | solution.py:418
  47.0 3.7 %third.1 = (f32[10,56,128]{2,1,0:T(8,128)S(1)}, f32[10,56,128]{2,1,0:T(8,128)S(1)}, f32[32,128]{1,0:T(8,128)S(1)}) custom-call(f32[2,32,128]{2,1,0:T(8,128)S(1)} %get-tuple-element.23.spread_in, f32[32,128]{1,0:T(8,128)S(1)} %collective-permute-done.3.got_a, f32[32,128]{1,0:T(8,128)S(1)} %slice_select_fusion.1.got_b, ...), custom_call_target="tpu_custom_call" | custom-call | tf_op jit(solution)/shard_map/third/pallas_call | solution.py:424
  50.7 16.0 %all_to_all.17 = f32[32,1,128]{2,1,0:T(1,128)S(1)} all-to-all(f32[32,1,128]{2,1,0:T(1,128)S(1)} %bitcast.46), channel_id=1, replica_groups=mesh['lat'=16,'lon'=32] {'lon'}, dimensions={0} | all-to-all | bytes 32768 | tf_op jit(solution)/shard_map/all_to_all | solution.py:428
  66.7 0.1 reduce_sum.9
  66.7 23.2 %all_to_all.18 = f32[16,1,128]{2,1,0:T(1,128)S(1)} all-to-all(f32[16,1,128]{2,1,0:T(1,128)S(1)} %broadcast_in_dim.2), channel_id=1, replica_groups=mesh['lat'=16,'lon'=32] {'lat'}, dimensions={0} | all-to-all | bytes 16384 | tf_op jit(solution)/shard_map/all_to_all | solution.py:430
  90.0 1.0 %last.1 = (f32[10,32,128]{2,1,0:T(8,128)}, f32[10,32,128]{2,1,0:T(8,128)}) custom-call(f32[16,128]{1,0:T(8,128)S(1)} %bitcast.45, f32[10,56,128]{2,1,0:T(8,128)S(1)} %get-tuple-element.30.x_first, f32[10,56,128]{2,1,0:T(8,128)S(1)} %get-tuple-element.31.y_first, f32[10,56,128]{2,1,0:T(8,128)S(1)} %get-tuple-element.32.x_second, ...), custom_call_target="tpu_custom_call" | custom-call | tf_op jit(solution)/shard_map/last/pallas_call | solution.py:431
  (18 shorter events, 0.1 us)
Async XLA Ops:
  1.3 0.9 copy-start
  2.2 0.9 %copy-start.2 = (f32[10,32,128]{2,1,0:T(8,128)S(1)}, f32[10,32,128]{2,1,0:T(8,128)}, u32[]{:S(2)}) copy-start(f32[10,32,128]{2,1,0:T(8,128)} %diffusivity_any.1) | copy-start | bytes 491524
  3.1 0.7 copy-start.3
  3.8 0.7 copy-start.4
  4.5 0.7 copy-start.5
  5.2 18.7 %copy-start.1 = (bf16[2,8,32,128]{3,2,1,0:T(8,128)(2,1)S(1)}, bf16[2,8,32,128]{3,2,1,0:T(8,128)(2,1)}, u32[]{:S(2)}) copy-start(bf16[2,8,32,128]{3,2,1,0:T(8,128)(2,1)} %param.8) | copy-start | bytes 393220
  6.1 10.4 %collective-permute-start = (f32[96,128]{1,0:T(8,128)S(1)}, f32[96,128]{1,0:T(8,128)S(1)}, u32[]{:S(2)}, u32[]{:S(2)}) collective-permute-start(f32[96,128]{1,0:T(8,128)S(1)} %get-tuple-element.19), channel_id=1, source_target_pairs={{0,31},{1,2},{2,1},{3,4},{4,3},{5,6},{6,5},{7,8},{8,7},{9,10},{10,... | collective-permute-start | bytes 147464 | tf_op jit(solution)/shard_map/ppermute | solution.py:405
  16.5 5.9 %collective-permute-start.2 = (f32[288,128]{1,0:T(8,128)S(1)}, f32[288,128]{1,0:T(8,128)S(1)}, u32[]{:S(2)}, u32[]{:S(2)}) collective-permute-start(f32[288,128]{1,0:T(8,128)S(1)} %get-tuple-element.36), channel_id=1, source_target_pairs={{32,0},{64,32},{96,64},{128,96},{160,128},{192,160},{224,192},{256... | collective-permute-start | bytes 442376 | tf_op jit(solution)/shard_map/ppermute | solution.py:418
  17.8 6.1 %collective-permute-start.1 = (f32[288,128]{1,0:T(8,128)S(1)}, f32[288,128]{1,0:T(8,128)S(1)}, u32[]{:S(2)}, u32[]{:S(2)}) collective-permute-start(f32[288,128]{1,0:T(8,128)S(1)} %get-tuple-element.37), channel_id=1, source_target_pairs={{0,32},{32,64},{64,96},{96,128},{128,160},{160,192},{192,224},{224... | collective-permute-start | bytes 442376 | tf_op jit(solution)/shard_map/ppermute | solution.py:417
  28.4 9.7 %collective-permute-start.3 = (f32[32,128]{1,0:T(8,128)S(1)}, f32[32,128]{1,0:T(8,128)S(1)}, u32[]{:S(2)}, u32[]{:S(2)}) collective-permute-start(f32[32,128]{1,0:T(8,128)S(1)} %get-tuple-element.24), channel_id=1, source_target_pairs={{0,31},{1,2},{2,1},{3,4},{4,3},{5,6},{6,5},{7,8},{8,7},{9,10},{10,... | collective-permute-start | bytes 49160 | tf_op jit(solution)/shard_map/ppermute | solution.py:405
  38.2 5.4 %collective-permute-start.4 = (f32[64,128]{1,0:T(8,128)S(1)}, f32[64,128]{1,0:T(8,128)S(1)}, u32[]{:S(2)}, u32[]{:S(2)}) collective-permute-start(f32[64,128]{1,0:T(8,128)S(1)} %pad_maximum_fusion), channel_id=1, source_target_pairs={{0,32},{32,64},{64,96},{96,128},{128,160},{160,192},{192,224},{224... | collective-permute-start | bytes 98312 | tf_op jit(solution)/shard_map/ppermute | solution.py:417
  42.3 4.7 %collective-permute-start.5 = (f32[64,128]{1,0:T(8,128)S(1)}, f32[64,128]{1,0:T(8,128)S(1)}, u32[]{:S(2)}, u32[]{:S(2)}) collective-permute-start(f32[64,128]{1,0:T(8,128)S(1)} %pad_maximum_fusion.1), channel_id=1, source_target_pairs={{32,0},{64,32},{96,64},{128,96},{160,128},{192,160},{224,192},{256... | collective-permute-start | bytes 98312 | tf_op jit(solution)/shard_map/ppermute | solution.py:418

commit v3 on v2

--- a/solution.py
+++ b/solution.py
@@ -20,9 +20,11 @@
 ALL = 2 * GROUP
 SLOT = 2 * HALO
 PACKS = 3
+PLANES = FIELDS + 2
 
 VMEM = pl.BlockSpec(memory_space=pltpu.VMEM)
-ANY = pl.BlockSpec(memory_space=pl.ANY)
+ANY = pl.BlockSpec(memory_space=pltpu.HBM)
+FIRST_LIMIT = 62 << 20
 PARAMS = pltpu.CompilerParams(vmem_limit_bytes=40 << 20)
 
 
@@ -75,7 +77,7 @@
 
 def first_kernel(
     odd_ref, diffusivity_any, mask_any, weights_any, innovation_any, precision_any, count_any,
-    base, send_a, send_b, start_vector, keep,
+    base, send_a, send_b,
     diffusivity, mask, weights, innovation, precision, count, sems,
 ):
     pairs = (
@@ -96,12 +98,12 @@
         for slot in range(OBS):
             at = f * OBS + slot
             kept = jnp.where(slot < valid, precision[f, 0, 0, slot], 0.0)
-            keep[at : at + 1] = jnp.full((1, COLS), kept, jnp.float32)
-            start_vector[at : at + 1] = jnp.full(
+            base[PLANES, 2 * OBS + at : 2 * OBS + at + 1] = jnp.full((1, COLS), kept, jnp.float32)
+            base[PLANES, at : at + 1] = jnp.full(
                 (1, COLS), kept * innovation[f, 0, 0, slot], jnp.float32
             )
-    vector = rounded(start_vector[...])
-    start_vector[...] = vector
+    vector = rounded(base[PLANES, : 2 * OBS])
+    base[PLANES, : 2 * OBS] = vector
     copies[3].wait()
     copies[4].wait()
     ocean = mask[...].astype(jnp.float32)
@@ -225,54 +227,55 @@
         for c in range(GROUP):
             at = f * GROUP + c
             if c < NCAT:
-                out_x[f * NCAT + c] = field[at]
+                k = f * NCAT + c
+                gather_rows(natural, k, field[at])
+                out_x[k] = natural[k, EDGE:-EDGE]
             field[at] = jnp.where(scaled[at] > 0.0, field[at], 0.0)
     diffuse(field, other, faces)
     totals = []
     for f in range(2):
-        total = jnp.zeros((DEEP, COLS), jnp.float32)
+        total = jnp.zeros((ROWS, COLS), jnp.float32)
         for c in range(NCAT):
-            at = f * GROUP + c
-            wet = jnp.where(scaled[at] > 0.0, field[at], 0.0)
-            out_y[f * NCAT + c] = wet
-            total = total + turn(wet, -HALO - SLOT * c)
-        gather_rows(natural, f, total)
-        totals.append(natural[f, EDGE:-EDGE])
+            at, k = f * GROUP + c, f * NCAT + c
+            gather_rows(natural, k, jnp.where(scaled[at] > 0.0, field[at], 0.0))
+            wet = turn(natural[k, EDGE:-EDGE], -HALO - SLOT * c)
+            out_y[k] = wet
+            total = total + wet
+        totals.append(total)
     return observe(weights, totals)
 
 
+def extend(natural, at, own, above, below, k):
+    natural[at, EDGE - HALO : EDGE] = above[k * HALO : (k + 1) * HALO]
+    natural[at, EDGE:-EDGE] = own
+    natural[at, EDGE + ROWS : EDGE + ROWS + HALO] = below[k * HALO : (k + 1) * HALO]
+
+
 def second_kernel(
-    odd_ref, base, got_a, got_b, above, below, weights, start_vector, keep,
+    odd_ref, base, sides, above, below, weights,
     out_x, out_y, scaled, faces, spread_out, send_a, send_b, vectors,
     natural, field, other,
 ):
     odd = odd_ref[0] == 1
-    planes = FIELDS + 2
-    strip = planes * EDGE
-    for k in range(planes):
-        f, c = divmod(k, NCAT)
-        at = f * GROUP + c
-        natural[at, :EDGE] = above[k * EDGE : (k + 1) * EDGE]
-        natural[at, EDGE:-EDGE] = base[k]
-        natural[at, -EDGE:] = below[k * EDGE : (k + 1) * EDGE]
-    for p in range(PACKS):
-        at = NCAT + GROUP * p
-        first = strip + p * EDGE
-        second = first + PACKS * EDGE
-        natural[at, :EDGE] = above[first : first + EDGE] + above[second : second + EDGE]
-        natural[at, EDGE:-EDGE] = (
-            got_a[p * ROWS : (p + 1) * ROWS] + got_b[p * ROWS : (p + 1) * ROWS]
-        )
-        natural[at, -EDGE:] = below[first : first + EDGE] + below[second : second + EDGE]
+    for k in range(FIELDS + 2 + PACKS):
+        if k < FIELDS + 2:
+            f, c = divmod(k, NCAT)
+            extend(natural, f * GROUP + c, base[k], above, below, k)
+        else:
+            p = k - FIELDS - 2
+            extend(natural, NCAT + GROUP * p, sides[p], above, below, k)
     for at in range(ALL):
         scaled[at] = deal(natural, at)
     make_faces(scaled, faces)
     for place, at in enumerate((2 * GROUP, 2 * GROUP + 1, 2 * GROUP + NCAT)):
         natural[place] = natural[at]
     seen = sweep(natural, scaled, faces, weights, out_x, out_y, field, other)
-    vector = rounded(keep[...] * seen)
+    keep = base[PLANES, 2 * OBS :]
+    vector = rounded(keep * seen)
     vectors[0] = seen
     vectors[1] = vector
+    vectors[2] = base[PLANES, : 2 * OBS]
+    vectors[3] = keep
     wet = turn(base[0], -HALO) > 0.0
     for f in range(2):
         spread_out[f] = turn(
@@ -282,24 +285,18 @@
 
 
 def third_kernel(
-    spread_in, got_a, got_b, above, below, weights, start_vector, keep,
+    spread_in, sides, above, below, weights,
     scaled, faces, vectors,
     out_x, out_y, sums,
     natural, field, other,
 ):
-    for f in range(2):
-        natural[f, :EDGE] = above[f * EDGE : (f + 1) * EDGE]
-        natural[f, EDGE:-EDGE] = spread_in[f]
-        natural[f, -EDGE:] = below[f * EDGE : (f + 1) * EDGE]
-    first, second = slice(2 * EDGE, 3 * EDGE), slice(3 * EDGE, 4 * EDGE)
-    natural[2, :EDGE] = above[first] + above[second]
-    natural[2, EDGE:-EDGE] = got_a[...] + got_b[...]
-    natural[2, -EDGE:] = below[first] + below[second]
+    for k in range(3):
+        extend(natural, k, spread_in[k] if k < 2 else sides[0], above, below, k)
     later = sweep(natural, scaled, faces, weights, out_x, out_y, field, other)
     seen = vectors[0]
     vector = vectors[1]
-    start = start_vector[...]
-    kept = keep[...]
+    start = vectors[2]
+    kept = vectors[3]
     terms = [
         start * seen, vector * seen, vector * later,
         seen * kept * seen, seen * kept * later, later * kept * later,
@@ -311,7 +308,7 @@
     sums[...] = jnp.broadcast_to(row, sums.shape)
 
 
-def last_kernel(sums, x_first, y_first, x_second, y_second, control, increment, natural):
+def last_kernel(sums, x_first, y_first, x_second, y_second, control, increment):
     row = jnp.sum(sums[...], axis=0, keepdims=True)
     lane = lanes(1)
     a, b, c, k00, k01, k11 = [
@@ -323,21 +320,18 @@
     share = 1.0 - alpha + beta
     below = (share * share * (1.0 + k00)) - 2.0 * share * alpha * (b + k01) + alpha * alpha * (c + k11)
     later = beta / below
-    first = jnp.broadcast_to(alpha + later * share, (DEEP, COLS))
-    second = jnp.broadcast_to(-later * alpha, (DEEP, COLS))
+    first = jnp.broadcast_to(alpha + later * share, (ROWS, COLS))
+    second = jnp.broadcast_to(-later * alpha, (ROWS, COLS))
     for k in range(FIELDS):
-        for place, (out, one, two) in enumerate(
-            ((control, x_first, x_second), (increment, y_first, y_second))
-        ):
-            at = 2 * k + place
-            gather_rows(natural, at, first * one[k] + second * two[k])
-            out[k] = turn(natural[at, EDGE:-EDGE], -HALO - SLOT * (k % NCAT))
-
-
-def call(kernel, name, outs, ins, scratch):
+        both = first * x_first[k] + second * x_second[k]
+        control[k] = turn(both, -HALO - SLOT * (k % NCAT))
+        increment[k] = first * y_first[k] + second * y_second[k]
+
+
+def call(kernel, name, outs, ins, scratch, params=PARAMS):
     return pl.pallas_call(
         kernel, out_shape=outs, in_specs=ins, out_specs=[VMEM] * len(outs),
-        scratch_shapes=scratch, compiler_params=PARAMS, name=name,
+        scratch_shapes=scratch, compiler_params=params, name=name,
     )
 
 
@@ -348,23 +342,23 @@
 def first_call():
     return call(
         first_kernel, "first",
-        (f32(FIELDS + 2, ROWS, COLS), f32(PACKS * ROWS, COLS), f32(PACKS * ROWS, COLS),
-         f32(2 * OBS, COLS), f32(2 * OBS, COLS)),
+        (f32(PLANES + 1, ROWS, COLS), f32(PACKS * ROWS, COLS), f32(PACKS * ROWS, COLS)),
         [SMEM] + [ANY] * 6,
         [pltpu.VMEM((FIELDS, ROWS, COLS), jnp.float32), pltpu.VMEM((ROWS, COLS), jnp.int32),
          pltpu.VMEM((2 * OBS, ROWS, COLS), jnp.bfloat16), pltpu.SMEM((2, 1, 1, OBS), jnp.float32),
          pltpu.SMEM((2, 1, 1, OBS), jnp.float32), pltpu.SMEM((1, 1), jnp.int32),
          pltpu.SemaphoreType.DMA((6,))],
+        pltpu.CompilerParams(vmem_limit_bytes=FIRST_LIMIT),
     )
 
 
 def second_call():
     return call(
         second_kernel, "second",
-        (f32(FIELDS, DEEP, COLS), f32(FIELDS, DEEP, COLS), f32(ALL, DEEP, COLS),
+        (f32(FIELDS, ROWS, COLS), f32(FIELDS, ROWS, COLS), f32(ALL, DEEP, COLS),
          f32(5, ALL, DEEP, COLS), f32(2, ROWS, COLS), f32(ROWS, COLS), f32(ROWS, COLS),
-         f32(2, 2 * OBS, COLS)),
-        [SMEM] + [VMEM] * 8,
+         f32(4, 2 * OBS, COLS)),
+        [SMEM] + [VMEM] * 5,
         [pltpu.VMEM((ALL + GROUP, TALL, COLS), jnp.float32)] + SWEEP,
     )
 
@@ -372,9 +366,9 @@
 def third_call(lon_count):
     return call(
         third_kernel, "third",
-        (f32(FIELDS, DEEP, COLS), f32(FIELDS, DEEP, COLS), f32(lon_count, COLS)),
-        [VMEM] * 11,
-        [pltpu.VMEM((3, TALL, COLS), jnp.float32)] + SWEEP,
+        (f32(FIELDS, ROWS, COLS), f32(FIELDS, ROWS, COLS), f32(lon_count, COLS)),
+        [VMEM] * 8,
+        [pltpu.VMEM((FIELDS, TALL, COLS), jnp.float32)] + SWEEP,
     )
 
 
@@ -383,7 +377,7 @@
         last_kernel, "last",
         (f32(FIELDS, ROWS, COLS), f32(FIELDS, ROWS, COLS)),
         [VMEM] * 5,
-        [pltpu.VMEM((2 * FIELDS, TALL, COLS), jnp.float32)],
+        [],
     )
 
 
@@ -397,33 +391,29 @@
     between = [(i, (i + 1 if i % 2 else i - 1) % lon_count) for i in range(lon_count)]
     weights = obs_weights.reshape(2 * OBS, ROWS, COLS)
 
-    base, send_a, send_b, start_vector, keep = first_call()(
+    base, send_a, send_b = first_call()(
         odd, diffusivity, land_mask, weights, innovation, precision_weights, obs_count
     )
 
     def exchange(planes, send_a, send_b):
         got_a = lax.ppermute(send_a, "lon", between)
         both = lax.all_gather(send_b, "lon", axis_index_groups=chips)
-        got_b = jnp.where(odd[0] == 1, both[0], both[1])
-        packs = send_a.shape[0] // ROWS
+        sides = got_a + jnp.where(odd[0] == 1, both[0], both[1])
+        sides = sides.reshape(-1, ROWS, COLS)
 
         def edge(at):
-            parts = [planes[:, at : at + EDGE].reshape(-1, COLS)]
-            for got in (got_a, got_b):
-                for pack in range(packs):
-                    parts.append(got[pack * ROWS + at : pack * ROWS + at + EDGE])
+            parts = [part[:, at : at + HALO].reshape(-1, COLS) for part in (planes, sides)]
             return jnp.concatenate(parts, axis=0)
 
-        above = lax.ppermute(edge(ROWS - EDGE), "lat", down)
+        above = lax.ppermute(edge(ROWS - HALO), "lat", down)
         below = lax.ppermute(edge(0), "lat", up)
-        return got_a, got_b, above, below
+        return sides, above, below
 
     x_first, y_first, scaled, faces, spread_first, send_a, send_b, vectors = second_call()(
-        odd, base, *exchange(base, send_a, send_b), weights, start_vector, keep
+        odd, base, *exchange(base[:PLANES], send_a, send_b), weights
     )
     x_second, y_second, sums = third_call(lon_count)(
-        spread_first, *exchange(spread_first, send_a, send_b), weights, start_vector, keep,
-        scaled, faces, vectors,
+        spread_first, *exchange(spread_first, send_a, send_b), weights, scaled, faces, vectors
     )
     sums = lax.all_to_all(sums, "lon", 0, 0, tiled=True)
     sums = jnp.broadcast_to(jnp.sum(sums, axis=0, keepdims=True), (lat_count, COLS))

time: 91.5 us -> 86 us (0.940)
  waiting for transfers between devices: 5.4 us -> 8.82 us
  local copies, waits for them, and re-layouts: 3.96 us -> 1.03 us
  starting transfers between devices: 17.2 us -> 14.3 us
  blocking collectives: 52.8 us -> 50.1 us
    ppermute x2, waiting for transfers between devices: 3.9 us -> 8.55 us  [exchange(): below = lax.ppermute(edge(0), 'lat', up)]
    unnamed x18 -> x4, local copies, waits for them, and re-layouts: 3.93 us -> 0.01 us
    ppermute x2, starting transfers between devices: 8.09 us -> 5.1 us  [exchange(): above = lax.ppermute(edge(ROWS - HALO), 'lat', down)]
    all_to_all x1, blocking collectives: 16 us -> 13.2 us  [per_device(): sums = lax.all_to_all(sums, 'lon', 0, 0, tiled=True)]
    ppermute x2, waiting for transfers between devices: 1.49 us -> 0.26 us  [exchange(): above = lax.ppermute(edge(ROWS - HALO), 'lat', down)]
    pallas_call x1, Pallas kernels: 0.87 us -> 1.88 us  [per_device(): first_call()]
    slice x4 -> x3, local copies, waits for them, and re-layouts: 0.02 us -> 0.98 us  [edge(): part[:, at:at + HALO].reshape(-1, COLS)]
  transfers between devices with their start and end apart: 6 -> 6, of which waited for: 3 -> 3; matrix products, arithmetic and copies ran while one was open for 0% -> 1% of each run, Pallas kernels for 0% -> 0%
where the time goes in v3:
time: 86 us; the launch traced here: 85.6 us
  blocking collectives  50.1 us (58%)
  starting transfers between devices  14.3 us (17%)
  Pallas kernels  9.73 us (11%)
  waiting for transfers between devices  8.82 us (10%)
  between operations  1.53 us (2%)
  local copies, waits for them, and re-layouts  1.03 us (1%)
    all_to_all x1, blocking collectives, per_device(): sums = lax.all_to_all(sums, 'lat', 0, 0, tiled=True)  24 us
    all_to_all x1, blocking collectives, per_device(): sums = lax.all_to_all(sums, 'lon', 0, 0, tiled=True)  13.2 us
    all_gather x2, blocking collectives, exchange(): both = lax.all_gather(send_b, 'lon', axis_index_groups=chips)  12.9 us
    ppermute x2, waiting for transfers between devices, exchange(): below = lax.ppermute(edge(0), 'lat', up)  8.55 us
    ppermute x2, starting transfers between devices, exchange(): got_a = lax.ppermute(send_a, 'lon', between)  6.64 us
    ppermute x2, starting transfers between devices, exchange(): above = lax.ppermute(edge(ROWS - HALO), 'lat', down)  5.1 us
    pallas_call x1, Pallas kernels, per_device(): second_call()(odd, base, *exchange(base[:PLANES], send_a, send_b), weights)  3.9 us
    pallas_call x1, Pallas kernels, per_device(): third_call(lon_count)  3.05 us
  transfers between devices with their start and end apart: 6, of which 3 were waited for; matrix products, arithmetic and copies ran while one was open for 1% of the time, Pallas kernels for 0%

profile of v3, /device:TPU:1, one launch (start us, length us, event | category | flops | bytes accessed | tf_op | source)
XLA Modules:
  0.0 85.6 jit_solution(16220385812906192464)
XLA Ops:
  0.6 0.0 copy-start
  1.3 1.9 %first.1 = (f32[13,32,128]{2,1,0:T(8,128)}, f32[96,128]{1,0:T(8,128)}, f32[96,128]{1,0:T(8,128)}) custom-call(s32[1]{0:T(128)} %bitcast.odd_ref, f32[10,32,128]{2,1,0:T(8,128)} %diffusivity_any.1, s32[32,128]{1,0:T(8,128)} %mask_any.1, bf16[16,32,128]{2,1,0:T(8,128)(2,1)} %bitcast.13, f32[2,1,1,8]{3,2,1,0:T(1,128)} %innovation_any.1, ...), custom_call_target="tpu_custom_call" | custom-call | tf_op jit(solution)/shard_map/first/pallas_call | solution.py:394
  3.2 0.0 copy-start.1
  3.2 4.7 %collective-permute-start = (f32[96,128]{1,0:T(8,128)}, f32[96,128]{1,0:T(8,128)S(1)}, u32[]{:S(2)}, u32[]{:S(2)}) collective-permute-start(f32[96,128]{1,0:T(8,128)} %get-tuple-element.17), channel_id=1, source_target_pairs={{0,31},{1,2},{2,1},{3,4},{4,3},{5,6},{6,5},{7,8},{8,7},{9,10},{10,... | collective-permute-start | bytes 147464 | tf_op jit(solution)/shard_map/ppermute | solution.py:399
  8.0 1.0 %fusion.3 = (f32[12,12,128]{2,1,0:T(8,128)S(1)}, f32[12,12,128]{2,1,0:T(8,128)S(1)}) fusion(f32[13,32,128]{2,1,0:T(8,128)} %get-tuple-element.16.base), kind=kLoop, calls=%fused_computation.11 | loop fusion | bytes 294912 | tf_op jit(solution)/shard_map/slice | solution.py:405
  9.0 5.9 %all-gather = f32[192,128]{1,0:T(8,128)S(1)} all-gather(f32[96,128]{1,0:T(8,128)} %get-tuple-element.18), channel_id=2, replica_groups={{0,1},{2,3},{4,5},{6,7},{8,9},{10,11},{12,13},{14,15},{16,17},{18,19},{..., dimensions={0}, use_global_device_ids=true | all-gather | bytes 147456 | tf_op jit(solution)/shard_map/all_gather | solution.py:400
  14.9 0.0 collective-permute-done
  15.0 2.8 %collective-permute-start.1 = (f32[180,128]{1,0:T(8,128)S(1)}, f32[180,128]{1,0:T(8,128)S(1)}, u32[]{:S(2)}, u32[]{:S(2)}) collective-permute-start(f32[180,128]{1,0:T(8,128)S(1)} %pad_maximum_fusion), channel_id=1, source_target_pairs={{0,32},{32,64},{64,96},{96,128},{128,160},{160,192},{192,224},{224... | collective-permute-start | bytes 276488 | tf_op jit(solution)/shard_map/ppermute | solution.py:408
  17.8 1.3 %collective-permute-start.2 = (f32[180,128]{1,0:T(8,128)S(1)}, f32[180,128]{1,0:T(8,128)S(1)}, u32[]{:S(2)}, u32[]{:S(2)}) collective-permute-start(f32[180,128]{1,0:T(8,128)S(1)} %pad_maximum_fusion.1), channel_id=1, source_target_pairs={{32,0},{64,32},{96,64},{128,96},{160,128},{192,160},{224,192},{256... | collective-permute-start | bytes 276488 | tf_op jit(solution)/shard_map/ppermute | solution.py:409
  19.1 0.3 collective-permute-done.1.above
  19.4 3.9 %collective-permute-done.2.below = f32[180,128]{1,0:T(8,128)S(1)} collective-permute-done((f32[180,128]{1,0:T(8,128)S(1)}, f32[180,128]{1,0:T(8,128)S(1)}, u32[]{:S(2)}, u32[]{:S(2)}) %collective-permute-start.2) | collective-permute-done | bytes 92192 | tf_op jit(solution)/shard_map/ppermute | solution.py:409
  23.3 0.0 copy-done
  23.3 0.0 copy-done.1
  23.3 3.9 %second.1 = (f32[10,32,128]{2,1,0:T(8,128)S(1)}, f32[10,32,128]{2,1,0:T(8,128)S(1)}, f32[12,56,128]{2,1,0:T(8,128)S(1)}, f32[5,12,56,128]{3,2,1,0:T(8,128)S(1)},...) custom-call(s32[1]{0:T(128)} %bitcast.odd_ref, ...), custom_call_target="tpu_custom_call" | custom-call | tf_op jit(solution)/shard_map/second/pallas_call | solution.py:412
  27.2 1.9 %collective-permute-start.3 = (f32[32,128]{1,0:T(8,128)S(1)}, f32[32,128]{1,0:T(8,128)S(1)}, u32[]{:S(2)}, u32[]{:S(2)}) collective-permute-start(f32[32,128]{1,0:T(8,128)S(1)} %get-tuple-element.20), channel_id=1, source_target_pairs={{0,31},{1,2},{2,1},{3,4},{4,3},{5,6},{6,5},{7,8},{8,7},{9,10},{10,... | collective-permute-start | bytes 49160 | tf_op jit(solution)/shard_map/ppermute | solution.py:399
  29.2 7.0 %all-gather.1 = f32[64,128]{1,0:T(8,128)S(1)} all-gather(f32[32,128]{1,0:T(8,128)S(1)} %get-tuple-element.21), channel_id=3, replica_groups={{0,1},{2,3},{4,5},{6,7},{8,9},{10,11},{12,13},{14,15},{16,17},{18,19},{..., dimensions={0}, use_global_device_ids=true | all-gather | bytes 49152 | tf_op jit(solution)/shard_map/all_gather | solution.py:400
  36.2 0.0 collective-permute-done.3
  36.2 2.3 %collective-permute-start.4 = (f32[36,128]{1,0:T(8,128)S(1)}, f32[36,128]{1,0:T(8,128)S(1)}, u32[]{:S(2)}, u32[]{:S(2)}) collective-permute-start(f32[36,128]{1,0:T(8,128)S(1)} %pad_maximum_fusion.2), channel_id=1, source_target_pairs={{0,32},{32,64},{64,96},{96,128},{128,160},{160,192},{192,224},{224... | collective-permute-start | bytes 55304 | tf_op jit(solution)/shard_map/ppermute | solution.py:408
  38.6 1.3 %collective-permute-start.5 = (f32[36,128]{1,0:T(8,128)S(1)}, f32[36,128]{1,0:T(8,128)S(1)}, u32[]{:S(2)}, u32[]{:S(2)}) collective-permute-start(f32[36,128]{1,0:T(8,128)S(1)} %pad_maximum_fusion.3), channel_id=1, source_target_pairs={{32,0},{64,32},{96,64},{128,96},{160,128},{192,160},{224,192},{256... | collective-permute-start | bytes 55304 | tf_op jit(solution)/shard_map/ppermute | solution.py:409
  39.9 0.0 collective-permute-done.4.above
  39.9 4.6 %collective-permute-done.5.below = f32[36,128]{1,0:T(8,128)S(1)} collective-permute-done((f32[36,128]{1,0:T(8,128)S(1)}, f32[36,128]{1,0:T(8,128)S(1)}, u32[]{:S(2)}, u32[]{:S(2)}) %collective-permute-start.5) | collective-permute-done | bytes 18464 | tf_op jit(solution)/shard_map/ppermute | solution.py:409
  44.5 3.0 %third.1 = (f32[10,32,128]{2,1,0:T(8,128)S(1)}, f32[10,32,128]{2,1,0:T(8,128)S(1)}, f32[32,128]{1,0:T(8,128)S(1)}) custom-call(f32[2,32,128]{2,1,0:T(8,128)S(1)} %get-tuple-element.19.spread_in, f32[1,32,128]{2,1,0:T(8,128)S(1)} %fusion.2.sides, f32[36,128]{1,0:T(8,128)S(1)} %collective-permute-done.4.above, f32[36,128]{1,0:T(8,128)S(1)} %collective-permute-done.5.below, ...), custom_call_target="tpu_custom_call" | custom-call | tf_op jit(solution)/shard_map/third/pallas_call | solution.py:415
  47.5 13.2 %all_to_all.17 = f32[32,1,128]{2,1,0:T(1,128)S(1)} all-to-all(f32[32,1,128]{2,1,0:T(1,128)S(1)} %bitcast.19), channel_id=1, replica_groups=mesh['lat'=16,'lon'=32] {'lon'}, dimensions={0} | all-to-all | bytes 32768 | tf_op jit(solution)/shard_map/all_to_all | solution.py:418
  60.7 0.1 reduce_sum.9
  60.7 24.0 %all_to_all.18 = f32[16,1,128]{2,1,0:T(1,128)S(1)} all-to-all(f32[16,1,128]{2,1,0:T(1,128)S(1)} %broadcast_in_dim.2), channel_id=1, replica_groups=mesh['lat'=16,'lon'=32] {'lat'}, dimensions={0} | all-to-all | bytes 16384 | tf_op jit(solution)/shard_map/all_to_all | solution.py:420
  84.7 0.9 %last.1 = (f32[10,32,128]{2,1,0:T(8,128)}, f32[10,32,128]{2,1,0:T(8,128)}) custom-call(f32[16,128]{1,0:T(8,128)S(1)} %bitcast.18, f32[10,32,128]{2,1,0:T(8,128)S(1)} %get-tuple-element.26.x_first, f32[10,32,128]{2,1,0:T(8,128)S(1)} %get-tuple-element.27.y_first, f32[10,32,128]{2,1,0:T(8,128)S(1)} %get-tuple-element.28.x_second, ...), custom_call_target="tpu_custom_call" | custom-call | tf_op jit(solution)/shard_map/last/pallas_call | solution.py:421
  (16 shorter events, 0.1 us)
Async XLA Ops:
  0.6 22.7 %copy-start = (bf16[2,8,32,128]{3,2,1,0:T(8,128)(2,1)S(1)}, bf16[2,8,32,128]{3,2,1,0:T(8,128)(2,1)}, u32[]{:S(2)}) copy-start(bf16[2,8,32,128]{3,2,1,0:T(8,128)(2,1)} %param.8) | copy-start | bytes 393220
  3.2 20.1 %copy-start.1 = (f32[13,32,128]{2,1,0:T(8,128)S(1)}, f32[13,32,128]{2,1,0:T(8,128)}, u32[]{:S(2)}) copy-start(f32[13,32,128]{2,1,0:T(8,128)} %get-tuple-element.16.base) | copy-start | bytes 638980
  3.2 11.7 %collective-permute-start = (f32[96,128]{1,0:T(8,128)}, f32[96,128]{1,0:T(8,128)S(1)}, u32[]{:S(2)}, u32[]{:S(2)}) collective-permute-start(f32[96,128]{1,0:T(8,128)} %get-tuple-element.17), channel_id=1, source_target_pairs={{0,31},{1,2},{2,1},{3,4},{4,3},{5,6},{6,5},{7,8},{8,7},{9,10},{10,... | collective-permute-start | bytes 147464 | tf_op jit(solution)/shard_map/ppermute | solution.py:399
  15.0 4.4 %collective-permute-start.1 = (f32[180,128]{1,0:T(8,128)S(1)}, f32[180,128]{1,0:T(8,128)S(1)}, u32[]{:S(2)}, u32[]{:S(2)}) collective-permute-start(f32[180,128]{1,0:T(8,128)S(1)} %pad_maximum_fusion), channel_id=1, source_target_pairs={{0,32},{32,64},{64,96},{96,128},{128,160},{160,192},{192,224},{224... | collective-permute-start | bytes 276488 | tf_op jit(solution)/shard_map/ppermute | solution.py:408
  17.8 5.5 %collective-permute-start.2 = (f32[180,128]{1,0:T(8,128)S(1)}, f32[180,128]{1,0:T(8,128)S(1)}, u32[]{:S(2)}, u32[]{:S(2)}) collective-permute-start(f32[180,128]{1,0:T(8,128)S(1)} %pad_maximum_fusion.1), channel_id=1, source_target_pairs={{32,0},{64,32},{96,64},{128,96},{160,128},{192,160},{224,192},{256... | collective-permute-start | bytes 276488 | tf_op jit(solution)/shard_map/ppermute | solution.py:409
  27.2 9.0 %collective-permute-start.3 = (f32[32,128]{1,0:T(8,128)S(1)}, f32[32,128]{1,0:T(8,128)S(1)}, u32[]{:S(2)}, u32[]{:S(2)}) collective-permute-start(f32[32,128]{1,0:T(8,128)S(1)} %get-tuple-element.20), channel_id=1, source_target_pairs={{0,31},{1,2},{2,1},{3,4},{4,3},{5,6},{6,5},{7,8},{8,7},{9,10},{10,... | collective-permute-start | bytes 49160 | tf_op jit(solution)/shard_map/ppermute | solution.py:399
  36.2 3.6 %collective-permute-start.4 = (f32[36,128]{1,0:T(8,128)S(1)}, f32[36,128]{1,0:T(8,128)S(1)}, u32[]{:S(2)}, u32[]{:S(2)}) collective-permute-start(f32[36,128]{1,0:T(8,128)S(1)} %pad_maximum_fusion.2), channel_id=1, source_target_pairs={{0,32},{32,64},{64,96},{96,128},{128,160},{160,192},{192,224},{224... | collective-permute-start | bytes 55304 | tf_op jit(solution)/shard_map/ppermute | solution.py:408
  38.6 5.9 %collective-permute-start.5 = (f32[36,128]{1,0:T(8,128)S(1)}, f32[36,128]{1,0:T(8,128)S(1)}, u32[]{:S(2)}, u32[]{:S(2)}) collective-permute-start(f32[36,128]{1,0:T(8,128)S(1)} %pad_maximum_fusion.3), channel_id=1, source_target_pairs={{32,0},{64,32},{96,64},{128,96},{160,128},{192,160},{224,192},{256... | collective-permute-start | bytes 55304 | tf_op jit(solution)/shard_map/ppermute | solution.py:409

commit v4 on v3

--- a/solution.py
+++ b/solution.py
@@ -155,10 +155,6 @@
     return ref[at, tile(t + 1)] if t + 1 < TILES else pltpu.roll(ref[at, tile(0)], 7, 0)
 
 
-def south_tile(ref, at, t):
-    return ref[at, tile(t - 1)] if t > 0 else pltpu.roll(ref[at, tile(TILES - 1)], 1, 0)
-
-
 def make_faces(scaled, faces):
     lane = lanes(8)
     for g in range(2):
@@ -172,41 +168,35 @@
             west = west_of(east, lane)
             for at, x, e, w in zip(places, here, east, west):
                 y = north_tile(scaled, at, t)
-                faces[1, at, tile(t)] = e
-                faces[2, at, tile(t)] = w
-                faces[3, at, tile(t)] = jnp.where((x > 0.0) & (y > 0.0), 0.5 * (x + y), 0.0)
-        for t in range(TILES):
-            for at in places:
-                south = south_tile(faces.at[3], at, t)
-                faces[4, at, tile(t)] = south
-                faces[0, at, tile(t)] = (
-                    1.0 - faces[1, at, tile(t)] - faces[2, at, tile(t)]
-                ) - (faces[3, at, tile(t)] + south)
+                faces[0, at, tile(t)] = e
+                faces[1, at, tile(t)] = w
+                faces[2, at, tile(t)] = jnp.where((x > 0.0) & (y > 0.0), 0.5 * (x + y), 0.0)
 
 
 def step(source, target, faces):
     lane = lanes(8)
-    for t in range(TILES):
-        for g in range(2):
-            places = [g * GROUP + c for c in range(GROUP)]
+    for g in range(2):
+        places = [g * GROUP + c for c in range(GROUP)]
+        north = {}
+        for at in places:
+            for t in range(TILES):
+                north[at, t] = faces[2, at, tile(t)] * (
+                    north_tile(source, at, t) - source[at, tile(t)]
+                )
+        for t in range(TILES):
             here = [source[at, tile(t)] for at in places]
             east = east_of(here, lane)
             west = west_of(here, lane)
             for at, x, e, w in zip(places, here, east, west):
-                along = faces[1, at, tile(t)] * e + faces[2, at, tile(t)] * w
-                across = faces[3, at, tile(t)] * north_tile(source, at, t) + faces[
-                    4, at, tile(t)
-                ] * south_tile(source, at, t)
-                target[at, tile(t)] = faces[0, at, tile(t)] * x + (along + across)
+                along = faces[0, at, tile(t)] * (e - x) + faces[1, at, tile(t)] * (w - x)
+                south = north[at, t - 1] if t > 0 else pltpu.roll(north[at, TILES - 1], 1, 0)
+                target[at, tile(t)] = x + (along + (north[at, t] - south))
 
 
 def diffuse(field, other, faces):
-    def two(_, carry):
+    for _ in range(STEPS // 2):
         step(field, other, faces)
         step(other, field, faces)
-        return carry
-
-    lax.fori_loop(0, STEPS // 2, two, 0)
 
 
 def sweep(natural, scaled, faces, weights, out_x, out_y, field, other):
@@ -356,7 +346,7 @@
     return call(
         second_kernel, "second",
         (f32(FIELDS, ROWS, COLS), f32(FIELDS, ROWS, COLS), f32(ALL, DEEP, COLS),
-         f32(5, ALL, DEEP, COLS), f32(2, ROWS, COLS), f32(ROWS, COLS), f32(ROWS, COLS),
+         f32(3, ALL, DEEP, COLS), f32(2, ROWS, COLS), f32(ROWS, COLS), f32(ROWS, COLS),
          f32(4, 2 * OBS, COLS)),
         [SMEM] + [VMEM] * 5,
         [pltpu.VMEM((ALL + GROUP, TALL, COLS), jnp.float32)] + SWEEP,
@@ -398,11 +388,12 @@
     def exchange(planes, send_a, send_b):
         got_a = lax.ppermute(send_a, "lon", between)
         both = lax.all_gather(send_b, "lon", axis_index_groups=chips)
+        planes, both = lax.optimization_barrier((planes, both))
         sides = got_a + jnp.where(odd[0] == 1, both[0], both[1])
         sides = sides.reshape(-1, ROWS, COLS)
 
         def edge(at):
-            parts = [part[:, at : at + HALO].reshape(-1, COLS) for part in (planes, sides)]
+            parts = [part[:, at : at + HALO].reshape(-1, COLS) for part in (planes[:PLANES], sides)]
             return jnp.concatenate(parts, axis=0)
 
         above = lax.ppermute(edge(ROWS - HALO), "lat", down)
@@ -410,7 +401,7 @@
         return sides, above, below
 
     x_first, y_first, scaled, faces, spread_first, send_a, send_b, vectors = second_call()(
-        odd, base, *exchange(base[:PLANES], send_a, send_b), weights
+        odd, base, *exchange(base, send_a, send_b), weights
     )
     x_second, y_second, sums = third_call(lon_count)(
         spread_first, *exchange(spread_first, send_a, send_b), weights, scaled, faces, vectors

time: 86 us -> 85.1 us (0.990)
  Pallas kernels: 9.73 us -> 8.86 us
where the time goes in v4:
time: 85.1 us; the launch traced here: 84.7 us
  blocking collectives  50.1 us (59%)
  starting transfers between devices  14.3 us (17%)
  Pallas kernels  8.86 us (10%)
  waiting for transfers between devices  8.82 us (10%)
  between operations  1.5 us (2%)
  local copies, waits for them, and re-layouts  1.02 us (1%)
    all_to_all x1, blocking collectives, per_device(): sums = lax.all_to_all(sums, 'lat', 0, 0, tiled=True)  24 us
    all_to_all x1, blocking collectives, per_device(): sums = lax.all_to_all(sums, 'lon', 0, 0, tiled=True)  13.2 us
    all_gather x2, blocking collectives, exchange(): both = lax.all_gather(send_b, 'lon', axis_index_groups=chips)  12.9 us
    ppermute x2, waiting for transfers between devices, exchange(): below = lax.ppermute(edge(0), 'lat', up)  8.55 us
    ppermute x2, starting transfers between devices, exchange(): got_a = lax.ppermute(send_a, 'lon', between)  6.51 us
    ppermute x2, starting transfers between devices, exchange(): above = lax.ppermute(edge(ROWS - HALO), 'lat', down)  5.24 us
    pallas_call x1, Pallas kernels, per_device(): second_call()(odd, base, *exchange(base, send_a, send_b), weights)  3.46 us
    pallas_call x1, Pallas kernels, per_device(): third_call(lon_count)  2.62 us
  transfers between devices with their start and end apart: 6, of which 3 were waited for; matrix products, arithmetic and copies ran while one was open for 1% of the time, Pallas kernels for 0%

profile of v4, /device:TPU:1, one launch (start us, length us, event | category | flops | bytes accessed | tf_op | source)
XLA Modules:
  0.0 84.7 jit_solution(7526278850282120378)
XLA Ops:
  1.3 1.9 %first.1 = (f32[13,32,128]{2,1,0:T(8,128)}, f32[96,128]{1,0:T(8,128)}, f32[96,128]{1,0:T(8,128)}) custom-call(s32[1]{0:T(128)} %bitcast.odd_ref, f32[10,32,128]{2,1,0:T(8,128)} %diffusivity_any.1, s32[32,128]{1,0:T(8,128)} %mask_any.1, bf16[16,32,128]{2,1,0:T(8,128)(2,1)} %bitcast.21, f32[2,1,1,8]{3,2,1,0:T(1,128)} %innovation_any.1, ...), custom_call_target="tpu_custom_call" | custom-call | tf_op jit(solution)/shard_map/first/pallas_call | solution.py:384
  3.2 4.6 %collective-permute-start = (f32[96,128]{1,0:T(8,128)}, f32[96,128]{1,0:T(8,128)S(1)}, u32[]{:S(2)}, u32[]{:S(2)}) collective-permute-start(f32[96,128]{1,0:T(8,128)} %get-tuple-element.21), channel_id=1, source_target_pairs={{0,31},{1,2},{2,1},{3,4},{4,3},{5,6},{6,5},{7,8},{8,7},{9,10},{10,... | collective-permute-start | bytes 147464 | tf_op jit(solution)/shard_map/ppermute | solution.py:389
  7.8 5.9 %all-gather = f32[192,128]{1,0:T(8,128)S(1)} all-gather(f32[96,128]{1,0:T(8,128)} %get-tuple-element.22), channel_id=2, replica_groups={{0,1},{2,3},{4,5},{6,7},{8,9},{10,11},{12,13},{14,15},{16,17},{18,19},{..., dimensions={0}, use_global_device_ids=true | all-gather | bytes 147456 | tf_op jit(solution)/shard_map/all_gather | solution.py:390
  13.7 1.0 %fusion.1 = (f32[12,12,128]{2,1,0:T(8,128)S(1)}, f32[12,12,128]{2,1,0:T(8,128)S(1)}) fusion(f32[13,32,128]{2,1,0:T(8,128)} %get-tuple-element.24.base), kind=kLoop, calls=%fused_computation.9 | loop fusion | bytes 294912 | tf_op jit(solution)/shard_map/slice | solution.py:396
  14.7 0.0 collective-permute-done
  14.8 0.0 copy-start.1
  14.8 0.0 copy-start
  14.8 2.9 %collective-permute-start.1 = (f32[180,128]{1,0:T(8,128)S(1)}, f32[180,128]{1,0:T(8,128)S(1)}, u32[]{:S(2)}, u32[]{:S(2)}) collective-permute-start(f32[180,128]{1,0:T(8,128)S(1)} %pad_maximum_fusion), channel_id=1, source_target_pairs={{0,32},{32,64},{64,96},{96,128},{128,160},{160,192},{192,224},{224... | collective-permute-start | bytes 276488 | tf_op jit(solution)/shard_map/ppermute | solution.py:399
  17.8 1.3 %collective-permute-start.2 = (f32[180,128]{1,0:T(8,128)S(1)}, f32[180,128]{1,0:T(8,128)S(1)}, u32[]{:S(2)}, u32[]{:S(2)}) collective-permute-start(f32[180,128]{1,0:T(8,128)S(1)} %pad_maximum_fusion.1), channel_id=1, source_target_pairs={{32,0},{64,32},{96,64},{128,96},{160,128},{192,160},{224,192},{256... | collective-permute-start | bytes 276488 | tf_op jit(solution)/shard_map/ppermute | solution.py:400
  19.1 0.3 collective-permute-done.1.above
  19.4 3.9 %collective-permute-done.2.below = f32[180,128]{1,0:T(8,128)S(1)} collective-permute-done((f32[180,128]{1,0:T(8,128)S(1)}, f32[180,128]{1,0:T(8,128)S(1)}, u32[]{:S(2)}, u32[]{:S(2)}) %collective-permute-start.2) | collective-permute-done | bytes 92192 | tf_op jit(solution)/shard_map/ppermute | solution.py:400
  23.3 0.0 copy-done.1
  23.3 0.0 copy-done
  23.3 3.5 %second.1 = (f32[10,32,128]{2,1,0:T(8,128)S(1)}, f32[10,32,128]{2,1,0:T(8,128)S(1)}, f32[12,56,128]{2,1,0:T(8,128)S(1)}, f32[3,12,56,128]{3,2,1,0:T(8,128)S(1)},...) custom-call(s32[1]{0:T(128)} %bitcast.odd_ref, ...), custom_call_target="tpu_custom_call" | custom-call | tf_op jit(solution)/shard_map/second/pallas_call | solution.py:403
  26.8 1.9 %collective-permute-start.3 = (f32[32,128]{1,0:T(8,128)S(1)}, f32[32,128]{1,0:T(8,128)S(1)}, u32[]{:S(2)}, u32[]{:S(2)}) collective-permute-start(f32[32,128]{1,0:T(8,128)S(1)} %get-tuple-element.26), channel_id=1, source_target_pairs={{0,31},{1,2},{2,1},{3,4},{4,3},{5,6},{6,5},{7,8},{8,7},{9,10},{10,... | collective-permute-start | bytes 49160 | tf_op jit(solution)/shard_map/ppermute | solution.py:389
  28.7 7.0 %all-gather.1 = f32[64,128]{1,0:T(8,128)S(1)} all-gather(f32[32,128]{1,0:T(8,128)S(1)} %get-tuple-element.27), channel_id=3, replica_groups={{0,1},{2,3},{4,5},{6,7},{8,9},{10,11},{12,13},{14,15},{16,17},{18,19},{..., dimensions={0}, use_global_device_ids=true | all-gather | bytes 49152 | tf_op jit(solution)/shard_map/all_gather | solution.py:390
  35.7 0.0 collective-permute-done.3
  35.8 2.3 %collective-permute-start.4 = (f32[36,128]{1,0:T(8,128)S(1)}, f32[36,128]{1,0:T(8,128)S(1)}, u32[]{:S(2)}, u32[]{:S(2)}) collective-permute-start(f32[36,128]{1,0:T(8,128)S(1)} %pad_maximum_fusion.2), channel_id=1, source_target_pairs={{0,32},{32,64},{64,96},{96,128},{128,160},{160,192},{192,224},{224... | collective-permute-start | bytes 55304 | tf_op jit(solution)/shard_map/ppermute | solution.py:399
  38.1 1.3 %collective-permute-start.5 = (f32[36,128]{1,0:T(8,128)S(1)}, f32[36,128]{1,0:T(8,128)S(1)}, u32[]{:S(2)}, u32[]{:S(2)}) collective-permute-start(f32[36,128]{1,0:T(8,128)S(1)} %pad_maximum_fusion.3), channel_id=1, source_target_pairs={{32,0},{64,32},{96,64},{128,96},{160,128},{192,160},{224,192},{256... | collective-permute-start | bytes 55304 | tf_op jit(solution)/shard_map/ppermute | solution.py:400
  39.4 0.0 collective-permute-done.4.above
  39.4 4.6 %collective-permute-done.5.below = f32[36,128]{1,0:T(8,128)S(1)} collective-permute-done((f32[36,128]{1,0:T(8,128)S(1)}, f32[36,128]{1,0:T(8,128)S(1)}, u32[]{:S(2)}, u32[]{:S(2)}) %collective-permute-start.5) | collective-permute-done | bytes 18464 | tf_op jit(solution)/shard_map/ppermute | solution.py:400
  44.0 2.6 %third.1 = (f32[10,32,128]{2,1,0:T(8,128)S(1)}, f32[10,32,128]{2,1,0:T(8,128)S(1)}, f32[32,128]{1,0:T(8,128)S(1)}) custom-call(f32[2,32,128]{2,1,0:T(8,128)S(1)} %get-tuple-element.29.spread_in, f32[1,32,128]{2,1,0:T(8,128)S(1)} %fusion.sides, f32[36,128]{1,0:T(8,128)S(1)} %collective-permute-done.4.above, f32[36,128]{1,0:T(8,128)S(1)} %collective-permute-done.5.below, ...), custom_call_target="tpu_custom_call" | custom-call | tf_op jit(solution)/shard_map/third/pallas_call | solution.py:406
  46.6 13.2 %all_to_all.17 = f32[32,1,128]{2,1,0:T(1,128)S(1)} all-to-all(f32[32,1,128]{2,1,0:T(1,128)S(1)} %bitcast.27), channel_id=1, replica_groups=mesh['lat'=16,'lon'=32] {'lon'}, dimensions={0} | all-to-all | bytes 32768 | tf_op jit(solution)/shard_map/all_to_all | solution.py:409
  59.8 0.1 reduce_sum.9
  59.9 24.0 %all_to_all.18 = f32[16,1,128]{2,1,0:T(1,128)S(1)} all-to-all(f32[16,1,128]{2,1,0:T(1,128)S(1)} %broadcast_in_dim.2), channel_id=1, replica_groups=mesh['lat'=16,'lon'=32] {'lat'}, dimensions={0} | all-to-all | bytes 16384 | tf_op jit(solution)/shard_map/all_to_all | solution.py:411
  83.8 0.9 %last.1 = (f32[10,32,128]{2,1,0:T(8,128)}, f32[10,32,128]{2,1,0:T(8,128)}) custom-call(f32[16,128]{1,0:T(8,128)S(1)} %bitcast.26, f32[10,32,128]{2,1,0:T(8,128)S(1)} %get-tuple-element.34.x_first, f32[10,32,128]{2,1,0:T(8,128)S(1)} %get-tuple-element.35.y_first, f32[10,32,128]{2,1,0:T(8,128)S(1)} %get-tuple-element.36.x_second, ...), custom_call_target="tpu_custom_call" | custom-call | tf_op jit(solution)/shard_map/last/pallas_call | solution.py:412
  (16 shorter events, 0.1 us)
Async XLA Ops:
  3.2 11.5 %collective-permute-start = (f32[96,128]{1,0:T(8,128)}, f32[96,128]{1,0:T(8,128)S(1)}, u32[]{:S(2)}, u32[]{:S(2)}) collective-permute-start(f32[96,128]{1,0:T(8,128)} %get-tuple-element.21), channel_id=1, source_target_pairs={{0,31},{1,2},{2,1},{3,4},{4,3},{5,6},{6,5},{7,8},{8,7},{9,10},{10,... | collective-permute-start | bytes 147464 | tf_op jit(solution)/shard_map/ppermute | solution.py:389
  14.8 8.5 %copy-start.1 = (f32[13,32,128]{2,1,0:T(8,128)S(1)}, f32[13,32,128]{2,1,0:T(8,128)}, u32[]{:S(2)}) copy-start(f32[13,32,128]{2,1,0:T(8,128)} %get-tuple-element.24.base) | copy-start | bytes 638980
  14.8 8.5 %copy-start = (bf16[2,8,32,128]{3,2,1,0:T(8,128)(2,1)S(1)}, bf16[2,8,32,128]{3,2,1,0:T(8,128)(2,1)}, u32[]{:S(2)}) copy-start(bf16[2,8,32,128]{3,2,1,0:T(8,128)(2,1)} %param.8) | copy-start | bytes 393220
  14.8 4.5 %collective-permute-start.1 = (f32[180,128]{1,0:T(8,128)S(1)}, f32[180,128]{1,0:T(8,128)S(1)}, u32[]{:S(2)}, u32[]{:S(2)}) collective-permute-start(f32[180,128]{1,0:T(8,128)S(1)} %pad_maximum_fusion), channel_id=1, source_target_pairs={{0,32},{32,64},{64,96},{96,128},{128,160},{160,192},{192,224},{224... | collective-permute-start | bytes 276488 | tf_op jit(solution)/shard_map/ppermute | solution.py:399
  17.8 5.5 %collective-permute-start.2 = (f32[180,128]{1,0:T(8,128)S(1)}, f32[180,128]{1,0:T(8,128)S(1)}, u32[]{:S(2)}, u32[]{:S(2)}) collective-permute-start(f32[180,128]{1,0:T(8,128)S(1)} %pad_maximum_fusion.1), channel_id=1, source_target_pairs={{32,0},{64,32},{96,64},{128,96},{160,128},{192,160},{224,192},{256... | collective-permute-start | bytes 276488 | tf_op jit(solution)/shard_map/ppermute | solution.py:400
  26.8 8.9 %collective-permute-start.3 = (f32[32,128]{1,0:T(8,128)S(1)}, f32[32,128]{1,0:T(8,128)S(1)}, u32[]{:S(2)}, u32[]{:S(2)}) collective-permute-start(f32[32,128]{1,0:T(8,128)S(1)} %get-tuple-element.26), channel_id=1, source_target_pairs={{0,31},{1,2},{2,1},{3,4},{4,3},{5,6},{6,5},{7,8},{8,7},{9,10},{10,... | collective-permute-start | bytes 49160 | tf_op jit(solution)/shard_map/ppermute | solution.py:389
  35.8 3.6 %collective-permute-start.4 = (f32[36,128]{1,0:T(8,128)S(1)}, f32[36,128]{1,0:T(8,128)S(1)}, u32[]{:S(2)}, u32[]{:S(2)}) collective-permute-start(f32[36,128]{1,0:T(8,128)S(1)} %pad_maximum_fusion.2), channel_id=1, source_target_pairs={{0,32},{32,64},{64,96},{96,128},{128,160},{160,192},{192,224},{224... | collective-permute-start | bytes 55304 | tf_op jit(solution)/shard_map/ppermute | solution.py:399
  38.1 5.9 %collective-permute-start.5 = (f32[36,128]{1,0:T(8,128)S(1)}, f32[36,128]{1,0:T(8,128)S(1)}, u32[]{:S(2)}, u32[]{:S(2)}) collective-permute-start(f32[36,128]{1,0:T(8,128)S(1)} %pad_maximum_fusion.3), channel_id=1, source_target_pairs={{32,0},{64,32},{96,64},{128,96},{160,128},{192,160},{224,192},{256... | collective-permute-start | bytes 55304 | tf_op jit(solution)/shard_map/ppermute | solution.py:400

commit v5 on v4

--- a/solution.py
+++ b/solution.py
@@ -77,7 +77,7 @@
 
 def first_kernel(
     odd_ref, diffusivity_any, mask_any, weights_any, innovation_any, precision_any, count_any,
-    base, send_a, send_b,
+    base, send_a, send_b, edges,
     diffusivity, mask, weights, innovation, precision, count, sems,
 ):
     pairs = (
@@ -115,6 +115,9 @@
     for f in range(2):
         strips(odd, [base[f * NCAT + c] for c in range(NCAT)], send_a, send_b, f * ROWS)
     strips(odd, [base[FIELDS], base[FIELDS + 1]], send_a, send_b, 2 * ROWS)
+    for k in range(PLANES):
+        edges[0, HALO * k : HALO * (k + 1)] = base[k, :HALO]
+        edges[1, HALO * k : HALO * (k + 1)] = base[k, ROWS - HALO :]
 
 
 def tile(t):
@@ -243,7 +246,7 @@
 
 def second_kernel(
     odd_ref, base, sides, above, below, weights,
-    out_x, out_y, scaled, faces, spread_out, send_a, send_b, vectors,
+    out_x, out_y, scaled, faces, spread_out, send_a, send_b, vectors, edges,
     natural, field, other,
 ):
     odd = odd_ref[0] == 1
@@ -272,6 +275,9 @@
             jnp.where(wet, spread(weights, vector, f), 0.0), HALO + SLOT * f
         )
     strips(odd, [spread_out[0], spread_out[1]], send_a, send_b, 0)
+    for f in range(2):
+        edges[0, HALO * f : HALO * (f + 1)] = spread_out[f, :HALO]
+        edges[1, HALO * f : HALO * (f + 1)] = spread_out[f, ROWS - HALO :]
 
 
 def third_kernel(
@@ -332,7 +338,8 @@
 def first_call():
     return call(
         first_kernel, "first",
-        (f32(PLANES + 1, ROWS, COLS), f32(PACKS * ROWS, COLS), f32(PACKS * ROWS, COLS)),
+        (f32(PLANES + 1, ROWS, COLS), f32(PACKS * ROWS, COLS), f32(PACKS * ROWS, COLS),
+         f32(2, HALO * PLANES, COLS)),
         [SMEM] + [ANY] * 6,
         [pltpu.VMEM((FIELDS, ROWS, COLS), jnp.float32), pltpu.VMEM((ROWS, COLS), jnp.int32),
          pltpu.VMEM((2 * OBS, ROWS, COLS), jnp.bfloat16), pltpu.SMEM((2, 1, 1, OBS), jnp.float32),
@@ -347,7 +354,7 @@
         second_kernel, "second",
         (f32(FIELDS, ROWS, COLS), f32(FIELDS, ROWS, COLS), f32(ALL, DEEP, COLS),
          f32(3, ALL, DEEP, COLS), f32(2, ROWS, COLS), f32(ROWS, COLS), f32(ROWS, COLS),
-         f32(4, 2 * OBS, COLS)),
+         f32(4, 2 * OBS, COLS), f32(2, 2 * HALO, COLS)),
         [SMEM] + [VMEM] * 5,
         [pltpu.VMEM((ALL + GROUP, TALL, COLS), jnp.float32)] + SWEEP,
     )
@@ -381,30 +388,31 @@
     between = [(i, (i + 1 if i % 2 else i - 1) % lon_count) for i in range(lon_count)]
     weights = obs_weights.reshape(2 * OBS, ROWS, COLS)
 
-    base, send_a, send_b = first_call()(
+    base, send_a, send_b, edges = first_call()(
         odd, diffusivity, land_mask, weights, innovation, precision_weights, obs_count
     )
 
-    def exchange(planes, send_a, send_b):
+    def exchange(edges, send_a, send_b):
         got_a = lax.ppermute(send_a, "lon", between)
         both = lax.all_gather(send_b, "lon", axis_index_groups=chips)
-        planes, both = lax.optimization_barrier((planes, both))
+        edges, both = lax.optimization_barrier((edges, both))
         sides = got_a + jnp.where(odd[0] == 1, both[0], both[1])
         sides = sides.reshape(-1, ROWS, COLS)
 
-        def edge(at):
-            parts = [part[:, at : at + HALO].reshape(-1, COLS) for part in (planes[:PLANES], sides)]
-            return jnp.concatenate(parts, axis=0)
-
-        above = lax.ppermute(edge(ROWS - HALO), "lat", down)
-        below = lax.ppermute(edge(0), "lat", up)
+        def edge(which, at):
+            return jnp.concatenate(
+                [edges[which], sides[:, at : at + HALO].reshape(-1, COLS)], axis=0
+            )
+
+        above = lax.ppermute(edge(1, ROWS - HALO), "lat", down)
+        below = lax.ppermute(edge(0, 0), "lat", up)
         return sides, above, below
 
-    x_first, y_first, scaled, faces, spread_first, send_a, send_b, vectors = second_call()(
-        odd, base, *exchange(base, send_a, send_b), weights
+    x_first, y_first, scaled, faces, spread_first, send_a, send_b, vectors, edges = second_call()(
+        odd, base, *exchange(edges, send_a, send_b), weights
     )
     x_second, y_second, sums = third_call(lon_count)(
-        spread_first, *exchange(spread_first, send_a, send_b), weights, scaled, faces, vectors
+        spread_first, *exchange(edges, send_a, send_b), weights, scaled, faces, vectors
     )
     sums = lax.all_to_all(sums, "lon", 0, 0, tiled=True)
     sums = jnp.broadcast_to(jnp.sum(sums, axis=0, keepdims=True), (lat_count, COLS))

time: 85.1 us -> 85.8 us (level)
  starting transfers between devices: 14.3 us -> 15.6 us
  local copies, waits for them, and re-layouts: 1.02 us -> 0.06 us
    ppermute x4, starting transfers between devices: 7.82 us -> 8.98 us  [the longest x2 6.39 us: exchange(): above = lax.ppermute(edge(1, ROWS - HALO), 'lat', down)]
    slice x3 -> x1, local copies, waits for them, and re-layouts: 0.97 us -> 0.01 us  [edge(): sides[:, at:at + HALO].reshape(-1, COLS)]
  transfers between devices with their start and end apart: 6 -> 6, of which waited for: 3 -> 3; matrix products, arithmetic and copies ran while one was open for 1% -> 0% of each run, Pallas kernels for 0% -> 0%
where the time goes in v5:
time: 85.8 us; the launch traced here: 85.5 us
  blocking collectives  49.8 us (58%)
  starting transfers between devices  15.6 us (18%)
  Pallas kernels  9.63 us (11%)
  waiting for transfers between devices  8.82 us (10%)
  between operations  1.47 us (2%)
    all_to_all x1, blocking collectives, per_device(): sums = lax.all_to_all(sums, 'lat', 0, 0, tiled=True)  23.9 us
    all_to_all x1, blocking collectives, per_device(): sums = lax.all_to_all(sums, 'lon', 0, 0, tiled=True)  13.1 us
    all_gather x2, blocking collectives, exchange(): both = lax.all_gather(send_b, 'lon', axis_index_groups=chips)  12.8 us
    ppermute x2, waiting for transfers between devices, exchange(): below = lax.ppermute(edge(0, 0), 'lat', up)  8.55 us
    ppermute x2, starting transfers between devices, exchange(): got_a = lax.ppermute(send_a, 'lon', between)  6.65 us
    ppermute x2, starting transfers between devices, exchange(): above = lax.ppermute(edge(1, ROWS - HALO), 'lat', down)  6.39 us
    pallas_call x1, Pallas kernels, per_device(): second_call()(odd, base, *exchange(edges, send_a, send_b), weights)  3.79 us
    pallas_call x1, Pallas kernels, per_device(): third_call(lon_count)  2.99 us
  transfers between devices with their start and end apart: 6, of which 3 were waited for; matrix products, arithmetic and copies ran while one was open for 0% of the time, Pallas kernels for 0%

profile of v5, /device:TPU:1, one launch (start us, length us, event | category | flops | bytes accessed | tf_op | source)
XLA Modules:
  0.0 85.5 jit_solution(6141914519555256448)
XLA Ops:
  1.3 2.0 %first.1 = (f32[13,32,128]{2,1,0:T(8,128)}, f32[96,128]{1,0:T(8,128)}, f32[96,128]{1,0:T(8,128)}, f32[2,144,128]{2,1,0:T(8,128)}) custom-call(s32[1]{0:T(128)} %bitcast.odd_ref, f32[10,32,128]{2,1,0:T(8,128)} %diffusivity_any.1, s32[32,128]{1,0:T(8,128)} %mask_any.1, bf16[16,32,128]{2,1,0:T(8,128)(2,1)} %bitcast.29, f32[2,1,1,8]{3,2,1,0:T(1,128)} %innovation_any.1, ...), custom_call_target="tpu_custom_call" | custom-call | tf_op jit(solution)/shard_map/first/pallas_call | solution.py:391
  3.3 0.0 copy-start.2
  3.3 4.7 %collective-permute-start = (f32[96,128]{1,0:T(8,128)}, f32[96,128]{1,0:T(8,128)S(1)}, u32[]{:S(2)}, u32[]{:S(2)}) collective-permute-start(f32[96,128]{1,0:T(8,128)} %get-tuple-element.23), channel_id=1, source_target_pairs={{0,31},{1,2},{2,1},{3,4},{4,3},{5,6},{6,5},{7,8},{8,7},{9,10},{10,... | collective-permute-start | bytes 147464 | tf_op jit(solution)/shard_map/ppermute | solution.py:396
  8.0 5.9 %all-gather = f32[192,128]{1,0:T(8,128)S(1)} all-gather(f32[96,128]{1,0:T(8,128)} %get-tuple-element.25), channel_id=2, replica_groups={{0,1},{2,3},{4,5},{6,7},{8,9},{10,11},{12,13},{14,15},{16,17},{18,19},{..., dimensions={0}, use_global_device_ids=true | all-gather | bytes 147456 | tf_op jit(solution)/shard_map/all_gather | solution.py:397
  13.9 0.0 copy-done.2
  14.0 0.0 collective-permute-done
  14.0 0.0 copy-start.1
  14.1 0.0 copy-start
  14.1 2.9 %collective-permute-start.1 = (f32[180,128]{1,0:T(8,128)S(1)}, f32[180,128]{1,0:T(8,128)S(1)}, u32[]{:S(2)}, u32[]{:S(2)}) collective-permute-start(f32[180,128]{1,0:T(8,128)S(1)} %pad_maximum_fusion), channel_id=1, source_target_pairs={{0,32},{32,64},{64,96},{96,128},{128,160},{160,192},{192,224},{224... | collective-permute-start | bytes 276488 | tf_op jit(solution)/shard_map/ppermute | solution.py:407
  17.0 1.3 %collective-permute-start.2 = (f32[180,128]{1,0:T(8,128)S(1)}, f32[180,128]{1,0:T(8,128)S(1)}, u32[]{:S(2)}, u32[]{:S(2)}) collective-permute-start(f32[180,128]{1,0:T(8,128)S(1)} %pad_maximum_fusion.1), channel_id=1, source_target_pairs={{32,0},{64,32},{96,64},{128,96},{160,128},{192,160},{224,192},{256... | collective-permute-start | bytes 276488 | tf_op jit(solution)/shard_map/ppermute | solution.py:408
  18.3 0.3 collective-permute-done.1.above
  18.6 3.9 %collective-permute-done.2.below = f32[180,128]{1,0:T(8,128)S(1)} collective-permute-done((f32[180,128]{1,0:T(8,128)S(1)}, f32[180,128]{1,0:T(8,128)S(1)}, u32[]{:S(2)}, u32[]{:S(2)}) %collective-permute-start.2) | collective-permute-done | bytes 92192 | tf_op jit(solution)/shard_map/ppermute | solution.py:408
  22.5 0.0 copy-done.1
  22.5 0.0 copy-done
  22.5 3.8 %second.1 = (f32[10,32,128]{2,1,0:T(8,128)S(1)}, f32[10,32,128]{2,1,0:T(8,128)S(1)}, f32[12,56,128]{2,1,0:T(8,128)S(1)}, f32[3,12,56,128]{3,2,1,0:T(8,128)S(1)},...) custom-call(s32[1]{0:T(128)} %bitcast.odd_ref, ...), custom_call_target="tpu_custom_call" | custom-call | tf_op jit(solution)/shard_map/second/pallas_call | solution.py:411
  26.3 1.9 %collective-permute-start.3 = (f32[32,128]{1,0:T(8,128)S(1)}, f32[32,128]{1,0:T(8,128)S(1)}, u32[]{:S(2)}, u32[]{:S(2)}) collective-permute-start(f32[32,128]{1,0:T(8,128)S(1)} %get-tuple-element.29), channel_id=1, source_target_pairs={{0,31},{1,2},{2,1},{3,4},{4,3},{5,6},{6,5},{7,8},{8,7},{9,10},{10,... | collective-permute-start | bytes 49160 | tf_op jit(solution)/shard_map/ppermute | solution.py:396
  28.3 6.8 %all-gather.1 = f32[64,128]{1,0:T(8,128)S(1)} all-gather(f32[32,128]{1,0:T(8,128)S(1)} %get-tuple-element.31), channel_id=3, replica_groups={{0,1},{2,3},{4,5},{6,7},{8,9},{10,11},{12,13},{14,15},{16,17},{18,19},{..., dimensions={0}, use_global_device_ids=true | all-gather | bytes 49152 | tf_op jit(solution)/shard_map/all_gather | solution.py:397
  35.1 0.0 collective-permute-done.3
  35.1 3.5 %collective-permute-start.4 = (f32[36,128]{1,0:T(8,128)S(1)}, f32[36,128]{1,0:T(8,128)S(1)}, u32[]{:S(2)}, u32[]{:S(2)}) collective-permute-start(f32[36,128]{1,0:T(8,128)S(1)} %pad_maximum_fusion.2), channel_id=1, source_target_pairs={{0,32},{32,64},{64,96},{96,128},{128,160},{160,192},{192,224},{224... | collective-permute-start | bytes 55304 | tf_op jit(solution)/shard_map/ppermute | solution.py:407
  38.6 1.3 %collective-permute-start.5 = (f32[36,128]{1,0:T(8,128)S(1)}, f32[36,128]{1,0:T(8,128)S(1)}, u32[]{:S(2)}, u32[]{:S(2)}) collective-permute-start(f32[36,128]{1,0:T(8,128)S(1)} %pad_maximum_fusion.3), channel_id=1, source_target_pairs={{32,0},{64,32},{96,64},{128,96},{160,128},{192,160},{224,192},{256... | collective-permute-start | bytes 55304 | tf_op jit(solution)/shard_map/ppermute | solution.py:408
  39.9 0.0 collective-permute-done.4.above
  39.9 4.6 %collective-permute-done.5.below = f32[36,128]{1,0:T(8,128)S(1)} collective-permute-done((f32[36,128]{1,0:T(8,128)S(1)}, f32[36,128]{1,0:T(8,128)S(1)}, u32[]{:S(2)}, u32[]{:S(2)}) %collective-permute-start.5) | collective-permute-done | bytes 18464 | tf_op jit(solution)/shard_map/ppermute | solution.py:408
  44.5 3.0 %third.1 = (f32[10,32,128]{2,1,0:T(8,128)S(1)}, f32[10,32,128]{2,1,0:T(8,128)S(1)}, f32[32,128]{1,0:T(8,128)S(1)}) custom-call(f32[2,32,128]{2,1,0:T(8,128)S(1)} %get-tuple-element.28.spread_in, f32[1,32,128]{2,1,0:T(8,128)S(1)} %fusion.sides, f32[36,128]{1,0:T(8,128)S(1)} %collective-permute-done.4.above, f32[36,128]{1,0:T(8,128)S(1)} %collective-permute-done.5.below, ...), custom_call_target="tpu_custom_call" | custom-call | tf_op jit(solution)/shard_map/third/pallas_call | solution.py:414
  47.5 13.1 %all_to_all.17 = f32[32,1,128]{2,1,0:T(1,128)S(1)} all-to-all(f32[32,1,128]{2,1,0:T(1,128)S(1)} %bitcast.35), channel_id=1, replica_groups=mesh['lat'=16,'lon'=32] {'lon'}, dimensions={0} | all-to-all | bytes 32768 | tf_op jit(solution)/shard_map/all_to_all | solution.py:417
  60.6 0.1 reduce_sum.9
  60.7 23.9 %all_to_all.18 = f32[16,1,128]{2,1,0:T(1,128)S(1)} all-to-all(f32[16,1,128]{2,1,0:T(1,128)S(1)} %broadcast_in_dim.2), channel_id=1, replica_groups=mesh['lat'=16,'lon'=32] {'lat'}, dimensions={0} | all-to-all | bytes 16384 | tf_op jit(solution)/shard_map/all_to_all | solution.py:419
  84.6 0.9 %last.1 = (f32[10,32,128]{2,1,0:T(8,128)}, f32[10,32,128]{2,1,0:T(8,128)}) custom-call(f32[16,128]{1,0:T(8,128)S(1)} %bitcast.34, f32[10,32,128]{2,1,0:T(8,128)S(1)} %get-tuple-element.38.x_first, f32[10,32,128]{2,1,0:T(8,128)S(1)} %get-tuple-element.39.y_first, f32[10,32,128]{2,1,0:T(8,128)S(1)} %get-tuple-element.40.x_second, ...), custom_call_target="tpu_custom_call" | custom-call | tf_op jit(solution)/shard_map/last/pallas_call | solution.py:420
  (13 shorter events, 0.1 us)
Async XLA Ops:
  3.3 10.7 %copy-start.2 = (f32[2,144,128]{2,1,0:T(8,128)S(1)}, f32[2,144,128]{2,1,0:T(8,128)}, u32[]{:S(2)}) copy-start(f32[2,144,128]{2,1,0:T(8,128)} %get-tuple-element.27) | copy-start | bytes 442372
  3.3 10.7 %collective-permute-start = (f32[96,128]{1,0:T(8,128)}, f32[96,128]{1,0:T(8,128)S(1)}, u32[]{:S(2)}, u32[]{:S(2)}) collective-permute-start(f32[96,128]{1,0:T(8,128)} %get-tuple-element.23), channel_id=1, source_target_pairs={{0,31},{1,2},{2,1},{3,4},{4,3},{5,6},{6,5},{7,8},{8,7},{9,10},{10,... | collective-permute-start | bytes 147464 | tf_op jit(solution)/shard_map/ppermute | solution.py:396
  14.0 8.5 %copy-start.1 = (f32[13,32,128]{2,1,0:T(8,128)S(1)}, f32[13,32,128]{2,1,0:T(8,128)}, u32[]{:S(2)}) copy-start(f32[13,32,128]{2,1,0:T(8,128)} %get-tuple-element.22.base) | copy-start | bytes 638980
  14.1 8.5 %copy-start = (bf16[2,8,32,128]{3,2,1,0:T(8,128)(2,1)S(1)}, bf16[2,8,32,128]{3,2,1,0:T(8,128)(2,1)}, u32[]{:S(2)}) copy-start(bf16[2,8,32,128]{3,2,1,0:T(8,128)(2,1)} %param.8) | copy-start | bytes 393220
  14.1 4.5 %collective-permute-start.1 = (f32[180,128]{1,0:T(8,128)S(1)}, f32[180,128]{1,0:T(8,128)S(1)}, u32[]{:S(2)}, u32[]{:S(2)}) collective-permute-start(f32[180,128]{1,0:T(8,128)S(1)} %pad_maximum_fusion), channel_id=1, source_target_pairs={{0,32},{32,64},{64,96},{96,128},{128,160},{160,192},{192,224},{224... | collective-permute-start | bytes 276488 | tf_op jit(solution)/shard_map/ppermute | solution.py:407
  17.0 5.5 %collective-permute-start.2 = (f32[180,128]{1,0:T(8,128)S(1)}, f32[180,128]{1,0:T(8,128)S(1)}, u32[]{:S(2)}, u32[]{:S(2)}) collective-permute-start(f32[180,128]{1,0:T(8,128)S(1)} %pad_maximum_fusion.1), channel_id=1, source_target_pairs={{32,0},{64,32},{96,64},{128,96},{160,128},{192,160},{224,192},{256... | collective-permute-start | bytes 276488 | tf_op jit(solution)/shard_map/ppermute | solution.py:408
  26.3 8.8 %collective-permute-start.3 = (f32[32,128]{1,0:T(8,128)S(1)}, f32[32,128]{1,0:T(8,128)S(1)}, u32[]{:S(2)}, u32[]{:S(2)}) collective-permute-start(f32[32,128]{1,0:T(8,128)S(1)} %get-tuple-element.29), channel_id=1, source_target_pairs={{0,31},{1,2},{2,1},{3,4},{4,3},{5,6},{6,5},{7,8},{8,7},{9,10},{10,... | collective-permute-start | bytes 49160 | tf_op jit(solution)/shard_map/ppermute | solution.py:396
  35.1 4.8 %collective-permute-start.4 = (f32[36,128]{1,0:T(8,128)S(1)}, f32[36,128]{1,0:T(8,128)S(1)}, u32[]{:S(2)}, u32[]{:S(2)}) collective-permute-start(f32[36,128]{1,0:T(8,128)S(1)} %pad_maximum_fusion.2), channel_id=1, source_target_pairs={{0,32},{32,64},{64,96},{96,128},{128,160},{160,192},{192,224},{224... | collective-permute-start | bytes 55304 | tf_op jit(solution)/shard_map/ppermute | solution.py:407
  38.6 5.9 %collective-permute-start.5 = (f32[36,128]{1,0:T(8,128)S(1)}, f32[36,128]{1,0:T(8,128)S(1)}, u32[]{:S(2)}, u32[]{:S(2)}) collective-permute-start(f32[36,128]{1,0:T(8,128)S(1)} %pad_maximum_fusion.3), channel_id=1, source_target_pairs={{32,0},{64,32},{96,64},{128,96},{160,128},{192,160},{224,192},{256... | collective-permute-start | bytes 55304 | tf_op jit(solution)/shard_map/ppermute | solution.py:408
